TPU v7x, 32 devices: a whole 2x2x4 slice. The times are simulated.
32 devices in a mesh: seq: 8 (over y, x, core), tp: 4 (over z).
Axes of the slice: x: 2, y: 2, z: 4, core: 2. Of those that a mesh axis runs over, the one named last changes fastest.
Arguments:
- layer_in: bfloat16 [2, 1024, 2048], P(None, 'seq'), may hold values from -6 to 6
- positions: int32 [2, 1024], P(None, 'seq'), may hold values from 0 to 4092, as said below
- first_gain: float32 [2048], replicated, may hold values from 0.5 to 1.5
- query_proj: bfloat16 [2048, 2048], P('seq', 'tp'), may hold values from -0.125 to 0.125
- key_projection: bfloat16 [2048, 1024], P('seq', 'tp'), may hold values from -0.125 to 0.125
- value_projection: bfloat16 [2048, 1024], P('seq', 'tp'), may hold values from -0.125 to 0.125
- gate_proj: bfloat16 [2048, 2048], P('seq', 'tp'), may hold values from -0.125 to 0.125
- output_proj: bfloat16 [2048, 2048], P('tp', 'seq'), may hold values from -1.5 to 1.5
- query_gain: float32 [128], replicated, may hold values from 0.5 to 1.5
- key_norm_gain: float32 [128], replicated, may hold values from 0.5 to 1.5
- second_gain: float32 [2048], replicated, may hold values from 0.5 to 1.5
- hidden_gate: bfloat16 [2048, 6144], P('tp', 'seq'), may hold values from -0.125 to 0.125
- hidden_up: bfloat16 [2048, 6144], P('tp', 'seq'), may hold values from -0.125 to 0.125
- hidden_down: bfloat16 [6144, 2048], P('seq', 'tp'), may hold values from -0.078125 to 0.078125
- out_cotangent: bfloat16 [2, 1024, 2048], P(None, ('seq', 'tp')), may hold values from -6 to 6
Outputs:
- layer_out: bfloat16 [2, 1024, 2048], P(None, ('seq', 'tp'))
- input_grad: float32 [2, 1024, 2048], P(None, ('seq', 'tp'))
- grad_firstgain: float32 [2048], replicated
- grad_query: float32 [2048, 2048], P('seq', 'tp')
- grad_keyproj: float32 [2048, 1024], P('seq', 'tp')
- grad_valueproj: float32 [2048, 1024], P('seq', 'tp')
- grad_gating: float32 [2048, 2048], P('seq', 'tp')
- grad_outproj: float32 [2048, 2048], P('tp', 'seq')
- grad_qgain: float32 [128], replicated
- grad_kgain: float32 [128], replicated
- grad_secondgain: float32 [2048], replicated
- grad_hgate: float32 [2048, 6144], P('tp', 'seq')
- grad_hup: float32 [2048, 6144], P('tp', 'seq')
- grad_hdown: float32 [6144, 2048], P('seq', 'tp')
Inputs may be any that keep to these rules, and one draw needn't show every extreme that they name: Within each micro-batch the first token has position 0, positions rise strictly from token to token, and the last token's position is 4092.
All inputs are finite; a program needn't handle non-finite values.
Results may differ from a plain program's by a relative error of at most 0.023.
Values may be sent and summed in bfloat16 or wider, within the bound.
No kernel may reach another device: no remote copies, remote signals or barrier semaphores. Data moves between devices by JAX's collectives and lax.ppermute only.
A program may use at most 192 MiB of HBM per device.

v0:
```python
import jax
import jax.numpy as jnp
from jax import lax
from jax.experimental import pallas as pl
from jax.experimental.pallas import tpu as pltpu
from jax.sharding import PartitionSpec as P

EPS = 1e-06
ROPE_BASE = 5000000.0
NEG_LARGE = -1e30
F32 = jnp.float32
LOW = jnp.bfloat16
VMEM_LIMIT = 60 * 1024 * 1024


def shape_of(shape, dtype):
    return jax.ShapeDtypeStruct(shape, dtype)


def run_kernel(body, outs, args, flops, scalars=None):
    moved = sum(a.size * a.dtype.itemsize for a in args)
    moved += sum(o.size * o.dtype.itemsize for o in outs)
    specs = [pl.BlockSpec(memory_space=pltpu.VMEM)] * len(args)
    if scalars is not None:
        specs = [pl.BlockSpec(memory_space=pltpu.SMEM)] + specs
        args = [scalars] + list(args)
    return pl.pallas_call(
        body,
        out_shape=outs,
        in_specs=specs,
        out_specs=[pl.BlockSpec(memory_space=pltpu.VMEM)] * len(outs),
        compiler_params=pltpu.CompilerParams(vmem_limit_bytes=VMEM_LIMIT),
        cost_estimate=pl.CostEstimate(
            flops=flops // 8, transcendentals=0, bytes_accessed=moved // 8
        ),
    )(*args)


def dot_nn(left, right):
    return jnp.dot(left, right, preferred_element_type=F32)


def dot_nt(left, right):
    return lax.dot_general(left, right, (((1,), (1,)), ((), ())), preferred_element_type=F32)


def dot_tn(left, right):
    return lax.dot_general(left, right, (((0,), (0,)), ((), ())), preferred_element_type=F32)


def rows_of(refs, place):
    return jnp.concatenate([refs[i][e] for i, e in (place[s] for s in range(len(place)))], axis=0)


def swap(value, axis, mask):
    count = lax.axis_size(axis)
    return lax.ppermute(value, axis, [(i, i ^ mask) for i in range(count)])


def gather_pieces(value, axis, order, hold=None, hold_last=None):
    pieces, place, slots = [value[None]], {0: (0, 0)}, [0]
    for mask in order[:-1]:
        sent = pieces[0] if len(pieces) == 1 else jnp.concatenate(pieces)
        if hold is not None and len(pieces) == 2:
            sent = after(sent, hold)
        last = slots
        pieces.append(swap(sent, axis, mask))
        got = [s ^ mask for s in slots]
        place.update({s: (len(pieces) - 1, i) for i, s in enumerate(got)})
        slots = slots + got
    received = pieces[-1] if hold_last is None else after(pieces[-1], hold_last)
    for piece, ids in ((sent, last), (received, got)):
        pieces.append(swap(piece, axis, order[-1]))
        place.update({s ^ order[-1]: (len(pieces) - 1, i) for i, s in enumerate(ids)})
    return pieces, place


def lane_order(order):
    return sorted(range(0, 2 << len(order), 2), key=lambda s: [s & mask for mask in order])


def sum_halves(keep, got, last):
    if last:
        return keep.astype(F32) + got.astype(F32)
    half = keep.shape[0] // 2
    sides = (slice(None, half), slice(half, None))
    return tuple((keep[at].astype(F32) + got[at].astype(F32)).astype(LOW) for at in sides)


def join_lanes(keep, send, last=False):
    return sum_halves(keep, swap(send, "seq", 1), last)


def scatter_step(halves, mask, last, hold=None):
    keep, send = halves
    got = swap(send, "seq", mask)
    if hold is not None:
        got = after(got, hold)
    return sum_halves(keep, got, last)


def scatter_lanes(total, order, hold=None):
    for mask in order:
        total = scatter_step(total, mask, mask == order[-1], hold if mask == order[0] else None)
    return total


def exchange_tp(blocks):
    return lax.all_to_all(blocks, "tp", 0, 0, tiled=True)


def spread_tp(value):
    count = lax.axis_size("tp")
    return exchange_tp(jnp.broadcast_to(value[None], (count,) + value.shape))


def after(value, *earlier):
    return lax.optimization_barrier((value, earlier))[0]


def tree_sum(terms):
    while len(terms) > 1:
        terms = [terms[i] + terms[i + 1] for i in range(0, len(terms), 2)]
    return terms[0]


def inverse_rms(value):
    return lax.rsqrt(jnp.mean(value * value, axis=-1, keepdims=True) + EPS)


def per_device(
    layer_in,
    positions,
    first_gain,
    query_proj,
    key_projection,
    value_projection,
    gate_proj,
    output_proj,
    query_gain,
    key_norm_gain,
    second_gain,
    hidden_gate,
    hidden_up,
    hidden_down,
    out_cotangent,
):
    micros, local_rows, width = layer_in.shape
    head = query_gain.shape[0]
    n = lax.axis_size("seq")
    p = lax.axis_size("tp")
    me_seq = lax.axis_index("seq")
    me_tp = lax.axis_index("tp")
    me = jnp.stack([me_seq, me_tp]).astype(jnp.int32)
    part = local_rows // p
    tokens = micros * local_rows
    ptok = micros * part
    block = width // n
    chunk = width // p
    q_width = query_proj.shape[1]
    kv_width = key_projection.shape[1]
    q_heads = q_width // head
    kv_heads = kv_width // head
    group = q_heads // kv_heads
    units = hidden_down.shape[0] // p
    half_a = units // 2 // 16 * 16
    half_b = units - half_a
    total_rows = local_rows * n
    scale = head ** (-0.5)
    masks = [1 << b for b in range((n - 1).bit_length())]
    go_a = masks[1:] + masks[:1]
    go_b = masks[:0:-1] + masks[:1]
    back_a = masks[1:]
    back_b = masks[:0:-1]
    even = list(range(0, n, 2))
    odd = list(range(1, n, 2))
    lane_a, lane_b = lane_order(back_a), lane_order(back_b)
    inner = block % 128 == 0

    def permute_columns(value):
        return jnp.concatenate(
            [
                lax.dynamic_slice_in_dim(value, (me_seq ^ j) * block, block, value.ndim - 1)
                for j in range(n)
            ],
            axis=-1,
        )

    def outer_permute(value):
        return value if inner else permute_columns(value)

    def read_permuted(ref, me_ref):
        if not inner:
            return ref[...]
        where = [pl.multiple_of((me_ref[0] ^ j) * block, block) for j in range(n)]
        return jnp.concatenate([ref[:, pl.ds(w, block)] for w in where], axis=1)

    def write_blocks(value, ref):
        for b in range(p):
            for m in range(micros):
                start = m * local_rows + b * part
                ref[b, m * part : (m + 1) * part, :] = value[start : start + part].astype(LOW)

    def read_blocks(ref):
        return jnp.concatenate(
            [ref[b, m * part : (m + 1) * part, :] for m in range(micros) for b in range(p)], axis=0
        )

    def sum_blocks(ref):
        return tree_sum([ref[b].astype(F32) for b in range(p)])

    block_out = shape_of((p, ptok, width), LOW)

    w3 = jnp.stack([hidden_gate.T, hidden_up.T, hidden_down]).reshape(3, p, units, chunk)
    w3 = w3.transpose(1, 0, 2, 3)

    w_q, q_place = gather_pieces(query_proj, "seq", go_a)
    w_kv, kv_place = gather_pieces(
        jnp.concatenate([key_projection, value_projection], axis=1), "seq", go_b
    )
    w_g, g_place = gather_pieces(gate_proj, "seq", go_a)
    w_o, o_place = gather_pieces(output_proj.T, "seq", go_b)
    steps = len(w_q)
    wire = exchange_tp(after(w3, w_q[1], w_kv[1]))
    cot_part = out_cotangent.reshape(ptok, width)
    cot = spread_tp(after(cot_part, wire)).reshape(tokens, width)

    x_part = lax.dynamic_slice_in_dim(layer_in, me_tp * part, part, 1)
    x_part = x_part.reshape(ptok, width).astype(F32)
    x_rows = outer_permute(layer_in.reshape(tokens, width))
    places = positions.reshape(tokens)
    gain_row = outer_permute(first_gain[None])
    middle_lane = head // 2
    inverse = jnp.exp(-(jnp.arange(middle_lane, dtype=F32) * 2.0 / head) * jnp.log(ROPE_BASE))
    angles = places.astype(F32)[:, None] * inverse[None, :]
    cosine = jnp.concatenate([jnp.cos(angles), jnp.cos(angles)], axis=-1)
    sine = jnp.concatenate([-jnp.sin(angles), jnp.sin(angles)], axis=-1)
    q_gain = query_gain[None]
    k_gain = key_norm_gain[None]

    def split_refs(refs, *counts):
        out = []
        for c in counts:
            out.append(refs[:c])
            refs = refs[c:]
        return out + [refs]

    def heads_forward(pre, gain, cos, sin):
        out = []
        for h in range(pre.shape[1] // head):
            u = pre[:, h * head : (h + 1) * head]
            y = u * inverse_rms(u) * gain
            out.append(y * cos + pltpu.roll(y, middle_lane, 1) * sin)
        return jnp.concatenate(out, axis=1)

    def heads_backward(grad, pre, gain, cos, sin):
        out = []
        gain_grad = jnp.zeros((1, head), F32)
        for h in range(pre.shape[1] // head):
            u = pre[:, h * head : (h + 1) * head]
            g = grad[:, h * head : (h + 1) * head]
            r = inverse_rms(u)
            unit = u * r
            y = g * cos + pltpu.roll(g * sin, middle_lane, 1)
            gain_grad = gain_grad + jnp.sum(y * unit, axis=0, keepdims=True)
            t = y * gain
            out.append(r * (t - unit * jnp.mean(t * unit, axis=-1, keepdims=True)))
        return jnp.concatenate(out, axis=1), gain_grad

    def qkv_body(me_ref, x, gain, cos, sin, qg, kg, *refs):
        wq, wkv, outs = split_refs(refs, steps, steps)
        normed_out, qpre_out, kpre_out, q_out, k_out, v_out = outs
        rows = read_permuted(x, me_ref).astype(F32)
        low = (rows * inverse_rms(rows) * read_permuted(gain, me_ref)).astype(LOW)
        normed_out[...] = low
        kv = dot_nn(low, rows_of(wkv, kv_place))
        key = kv[:, :kv_width]
        kpre_out[...] = key
        v_out[...] = kv[:, kv_width:].astype(LOW)
        k_out[...] = heads_forward(key, kg[...], cos[...], sin[...]).astype(LOW)
        query = dot_nn(low, rows_of(wq, q_place))
        qpre_out[...] = query
        q_out[...] = heads_forward(query, qg[...], cos[...], sin[...]).astype(LOW)

    normed, query_pre, key_pre, query_low, key_low, value_low = run_kernel(
        qkv_body,
        [
            shape_of((tokens, width), LOW),
            shape_of((tokens, q_width), F32),
            shape_of((tokens, kv_width), F32),
            shape_of((tokens, q_width), LOW),
            shape_of((tokens, kv_width), LOW),
            shape_of((tokens, kv_width), LOW),
        ],
        [after(x_rows, w_g[1], w_o[1]), gain_row, cosine, sine, q_gain, k_gain, *w_q, *w_kv],
        2 * tokens * width * (q_width + 2 * kv_width),
        me,
    )
    keys, key_place = gather_pieces(key_low, "seq", go_a)
    values, value_place = gather_pieces(value_low, "seq", go_b)

    f_own = wire.transpose(1, 2, 0, 3).reshape(3, units, width)
    f_own = after(f_own, keys[-1], values[-1], w_g[-1], w_o[-1])

    inside = jnp.arange(local_rows, dtype=jnp.int32)
    query_pos = jnp.tile(me_seq * local_rows + inside, group)[:, None]
    key_pos = jnp.concatenate([(me_seq ^ j) * local_rows + inside for j in range(n)])[None, :]

    def group_rows(value, m, g):
        rows = value[m * local_rows : (m + 1) * local_rows]
        heads = range(g * group, (g + 1) * group)
        return jnp.concatenate([rows[:, h * head : (h + 1) * head] for h in heads], axis=0)

    def slot_rows(refs, place, m, g):
        rows = []
        for j in range(n):
            index, entry = place[j]
            start = m * local_rows
            at = (entry, slice(start, start + local_rows), slice(g * head, (g + 1) * head))
            rows.append(refs[index][at])
        return jnp.concatenate(rows, axis=0)

    def softmax_of(query, key, qpos, kpos):
        scores = jnp.where(kpos <= qpos, dot_nt(query, key) * scale, NEG_LARGE)
        weights = jnp.exp(scores - jnp.max(scores, axis=-1, keepdims=True))
        return weights * (1.0 / jnp.sum(weights, axis=-1, keepdims=True))

    def ungroup(pieces):
        rows = []
        for m in range(micros):
            columns = []
            for g in range(kv_heads):
                value = pieces[m, g]
                columns += [
                    value[h * local_rows : (h + 1) * local_rows] for h in range(group)
                ]
            rows.append(jnp.concatenate(columns, axis=1))
        return jnp.concatenate(rows, axis=0)

    def attend_body(q, normed_ref, qpos, kpos, *refs):
        ks, vs, wg, wo, outs = split_refs(refs, steps, steps, steps, steps)
        gate_out, att_out, gated_out, send_out = outs
        gate = dot_nn(normed_ref[...], rows_of(wg, g_place))
        gate_out[...] = gate
        query = q[...]
        pieces = {}
        for m in range(micros):
            for g in range(kv_heads):
                prob = softmax_of(
                    group_rows(query, m, g), slot_rows(ks, key_place, m, g), qpos[...], kpos[...]
                )
                pieces[m, g] = dot_nn(prob.astype(LOW), slot_rows(vs, value_place, m, g))
        att = ungroup(pieces)
        att_out[...] = att
        gated = (att * jax.nn.sigmoid(gate)).astype(LOW)
        gated_out[...] = gated
        write_blocks(dot_nt(gated, rows_of(wo, o_place)), send_out)

    att_flops = 4 * tokens * total_rows * q_width
    gate_pre, attended, gated_low, send = run_kernel(
        attend_body,
        [
            shape_of((tokens, q_width), F32),
            shape_of((tokens, q_width), F32),
            shape_of((tokens, q_width), LOW),
            block_out,
        ],
        [after(query_low, wire), normed, query_pos, key_pos, *keys, *values, *w_g, *w_o],
        att_flops + 4 * tokens * width * q_width,
    )
    got = exchange_tp(after(send, cot))

    def middle_body(me_ref, x, gain, got_ref, middle_out, low_out, total_ref):
        total_ref[...] = sum_blocks(got_ref)
        rows = x[...] + read_permuted(total_ref, me_ref)
        middle_out[...] = rows
        low = (rows * inverse_rms(rows) * gain[...]).astype(LOW)
        for b in range(p):
            low_out[b] = low

    def run_part(body, outs, args):
        specs = [pl.BlockSpec(memory_space=pltpu.SMEM)]
        specs += [pl.BlockSpec(memory_space=pltpu.VMEM)] * len(args)
        return pl.pallas_call(
            body,
            out_shape=outs,
            in_specs=specs,
            out_specs=[pl.BlockSpec(memory_space=pltpu.VMEM)] * len(outs),
            scratch_shapes=[pltpu.VMEM((ptok, width), F32)],
            compiler_params=pltpu.CompilerParams(vmem_limit_bytes=VMEM_LIMIT),
            cost_estimate=pl.CostEstimate(
                flops=20 * ptok * width, transcendentals=0, bytes_accessed=20 * ptok * width
            ),
        )(me, *args)

    part_f32 = shape_of((ptok, width), F32)
    gain_f32 = shape_of((1, width), F32)
    second = second_gain[None]
    middle, normed_two = run_part(
        middle_body,
        [part_f32, block_out],
        [x_part, second, outer_permute(got)],
    )
    n2 = exchange_tp(normed_two).reshape(tokens, width)
    f_a, fa_place = gather_pieces(f_own[:, :half_a], "seq", go_a, send, n2)
    f_b, fb_place = gather_pieces(f_own[:, half_a:], "seq", go_b, send, n2)

    lanes = n // 2
    halves = (half_a, half_b)
    lane_units = lanes * units
    pair = 2 if lanes % 2 == 0 else 1
    anywhere = pl.BlockSpec(memory_space=pl.ANY)
    whole = pl.BlockSpec(memory_space=pltpu.VMEM)
    f_places = (fa_place, fb_place)

    def start_loads(slots, refs, skipped, w, sem):
        count = len(refs) // 2
        loads = []
        for s, slot in enumerate(slots):
            for t in range(2):
                index, entry = f_places[t][slot]
                where = pl.ds(s * units + t * half_a, halves[t])
                source = refs[t * count + index - skipped].at[entry]
                copy = pltpu.make_async_copy(source, w.at[:, where, :], sem.at[2 * s + t])
                copy.start()
                loads.append(copy)
        return loads

    def pair_rows(step, loads):
        for copy in loads[2 * pair * step : 2 * pair * (step + 1)]:
            copy.wait()
        return slice(step * pair * units, (step + 1) * pair * units)

    def forward_body(last, slots, count, x, *refs):
        held, before, outs, (w, sem) = split_refs(refs, 2 * count, 1 if last else 0, 4)
        loads = start_loads(slots, held, steps - 2 if last else 0, w, sem)
        for step in range(lanes // pair):
            rows = pair_rows(step, loads)
            gate = dot_nt(w[0, rows], x[...])
            up = dot_nt(w[1, rows], x[...])
            outs[0][rows] = gate
            outs[1][rows] = up
            outs[2][rows] = (gate * jax.nn.sigmoid(gate) * up).astype(LOW)
        out = dot_tn(outs[2][...], w[2])
        if last:
            out = out + before[0][...]
        outs[3][...] = out.astype(outs[3].dtype)

    def run_forward(last, dtype, slots, *before):
        use = slice(steps - 2, steps) if last else slice(0, steps - 2)
        held = [*f_a[use], *f_b[use]]
        return pl.pallas_call(
            lambda *r: forward_body(last, slots, len(held) // 2, *r),
            out_shape=[
                shape_of((lane_units, tokens), F32),
                shape_of((lane_units, tokens), F32),
                shape_of((lane_units, tokens), LOW),
                shape_of((tokens, width), dtype),
            ],
            in_specs=[whole] + [anywhere] * len(held) + [whole] * len(before),
            out_specs=[whole] * 4,
            scratch_shapes=[
                pltpu.VMEM((3, lane_units, width), LOW),
                pltpu.SemaphoreType.DMA((2 * lanes,)),
            ],
            compiler_params=pltpu.CompilerParams(vmem_limit_bytes=VMEM_LIMIT),
            cost_estimate=pl.CostEstimate(
                flops=6 * tokens * width * lane_units // 8,
                transcendentals=0,
                bytes_accessed=(6 * lane_units * width + 4 * tokens * width) // 8,
            ),
        )(n2, *held, *before)

    *acts_even, out_even = run_forward(False, F32, even)
    *acts_odd, out_sum = run_forward(True, LOW, odd, out_even)
    out_got = exchange_tp(out_sum.reshape(p, ptok, width))

    def backward_body(first, slots, count, x, c, gate_ref, up_ref, hid_ref, *refs):
        held, before, grads, (acc,), scratch = split_refs(
            refs, 2 * count, 0 if first else 1, 6, 1
        )
        w, low = scratch[:2]
        gbufs, in_sem, out_sem = scratch[2:8], scratch[8], scratch[9]
        loads = start_loads(slots, held, steps - 2 if first else 0, w, in_sem)
        stores = []

        def store(k, step, value):
            t, h = k % 2, halves[k % 2]
            for q in range(pair):
                slot = slots[step * pair + q] & ~1
                start = (lane_a, lane_b)[t].index(slot) * h
                at = pl.ds(start, h)
                source = q * units + t * half_a
                gbufs[k][start : start + h] = value[source : source + h]
                copy = pltpu.make_async_copy(
                    gbufs[k].at[at], grads[k].at[at], out_sem.at[6 * (step * pair + q) + k]
                )
                copy.start()
                stores.append(copy)

        for step in range(lanes // pair):
            rows = pair_rows(step, loads)
            gate, up = gate_ref[rows], up_ref[rows]
            grad = dot_nt(w[2, rows], c[...])
            sig = jax.nn.sigmoid(gate)
            gate_grad = (grad * up * sig * (1.0 + gate * (1.0 - sig))).astype(LOW)
            up_grad = (grad * gate * sig).astype(LOW)
            low[0, rows] = gate_grad
            low[1, rows] = up_grad
            sides = ((hid_ref[rows], c), (gate_grad, x), (up_grad, x))
            for i, (left, right) in zip((2, 0, 1), sides):
                value = dot_nn(left, right[...]).astype(LOW)
                store(2 * i, step, value)
                store(2 * i + 1, step, value)
        back = dot_tn(low[0], w[0]) + dot_tn(low[1], w[1])
        if not first:
            back = back + before[0][...]
        acc[...] = back.astype(acc.dtype)
        for copy in stores:
            copy.wait()

    def run_backward(first, dtype, slots, acts, *before):
        grad_outs = [shape_of((lanes * h, width), LOW) for _ in range(3) for h in halves]
        use = slice(steps - 2, steps) if first else slice(0, steps - 2)
        held = [*f_a[use], *f_b[use]]
        return pl.pallas_call(
            lambda *r: backward_body(first, slots, len(held) // 2, *r),
            out_shape=grad_outs + [shape_of((tokens, width), dtype)],
            in_specs=[whole] * 5 + [anywhere] * len(held) + [whole] * len(before),
            out_specs=[anywhere] * 6 + [whole],
            scratch_shapes=[
                pltpu.VMEM((3, lane_units, width), LOW),
                pltpu.VMEM((2, lane_units, tokens), LOW),
                *[pltpu.VMEM((lanes * h, width), LOW) for _ in range(3) for h in halves],
                pltpu.SemaphoreType.DMA((2 * lanes,)),
                pltpu.SemaphoreType.DMA((6 * lanes,)),
            ],
            compiler_params=pltpu.CompilerParams(vmem_limit_bytes=VMEM_LIMIT),
            cost_estimate=pl.CostEstimate(
                flops=12 * tokens * width * lane_units // 8,
                transcendentals=0,
                bytes_accessed=(12 * lane_units * width + 8 * tokens * width) // 8,
            ),
        )(n2, cot, *acts, *held, *before)

    *f_odd, back_odd = run_backward(True, F32, odd, acts_odd)
    *f_even, back_sum = run_backward(False, LOW, even, acts_even, back_odd)
    back_got = exchange_tp(after(back_sum, out_got).reshape(p, ptok, width))
    orders = (back_a, back_b)

    def first_steps(index):
        return [join_lanes(f_even[2 * index + t], f_odd[2 * index + t]) for t in range(2)]

    def next_steps(states, level, hold=None):
        last = level == len(back_a) - 1
        return [
            scatter_step(state, orders[t][level], last, hold) for t, state in enumerate(states)
        ]

    def last_steps(states, level, hold=None):
        for k in range(level, len(back_a)):
            states = next_steps(states, k, hold)
        return states

    def return_units(states, hold):
        blocks = jnp.concatenate(states).astype(LOW)
        blocks = blocks.reshape(units, p, chunk).transpose(1, 0, 2)
        raw = exchange_tp(after(blocks, hold))
        return raw, raw.reshape(p * units, chunk).astype(F32)

    down, gates, ups = first_steps(2), first_steps(0), first_steps(1)
    down = next_steps(down, 0)

    def branch_body(me_ref, mid, cot_ref, gain, got_ref, mg_out, low_out, gain_out, scratch):
        total = sum_blocks(got_ref)
        rows = mid[...]
        r = inverse_rms(rows)
        unit = rows * r
        gain_out[...] = jnp.sum(total * unit, axis=0, keepdims=True)
        u = total * gain[...]
        grad = cot_ref[...].astype(F32) + r * (u - unit * jnp.mean(u * unit, -1, keepdims=True))
        mg_out[...] = grad
        scratch[...] = grad
        low = read_permuted(scratch, me_ref).astype(LOW)
        for b in range(p):
            low_out[b] = low

    middle_grad, branch_low, grad_second = run_part(
        branch_body,
        [part_f32, block_out, gain_f32],
        [middle, cot_part, second, back_got],
    )
    branch_grad = exchange_tp(outer_permute(branch_low))
    gates = next_steps(gates, 0, branch_low)
    ups = [after(u, *down) for u in ups]
    down_last = last_steps(down, 1, branch_low)
    down_raw, grad_hdown = return_units(down_last, branch_grad)

    def back_body(q, qpre, gate, att, cos, sin, qg, qpos, kpos, *refs):
        ks, vs, wo, (bg,), outs = split_refs(refs, steps, steps, steps, 1)
        k_odd, k_even, v_odd, v_even, dq_out, dg_out, bg_out, gain_out = outs
        branch = read_blocks(bg)
        bg_out[...] = branch
        gated_grad = dot_nn(branch, rows_of(wo, o_place))
        sig = jax.nn.sigmoid(gate[...])
        att_grad = (gated_grad * sig).astype(LOW)
        dg_out[...] = (gated_grad * att[...] * sig * (1.0 - sig)).astype(LOW)
        product = att_grad.astype(F32) * att[...]
        query = q[...]
        pieces = {}
        for m in range(micros):
            for g in range(kv_heads):
                qr = group_rows(query, m, g)
                ag = group_rows(att_grad, m, g)
                key = slot_rows(ks, key_place, m, g)
                value = slot_rows(vs, value_place, m, g)
                delta = jnp.sum(group_rows(product, m, g), axis=-1, keepdims=True)
                prob = softmax_of(qr, key, qpos[...], kpos[...])
                ds = (prob * (dot_nt(ag, value) - delta)).astype(LOW)
                pieces[m, g] = dot_nn(ds, key) * scale
                dk = dot_tn(ds, qr).astype(LOW)
                dv = dot_tn(prob.astype(LOW), ag).astype(LOW)
                for j in range(n):
                    src = slice(j * local_rows, (j + 1) * local_rows)
                    pairs = ((k_odd, k_even, lane_a, dk), (v_odd, v_even, lane_b, dv))
                    for odd_ref, even_ref, lane, value_grad in pairs:
                        dst = lane.index(j & ~1) * tokens + m * local_rows
                        at = (slice(dst, dst + local_rows), slice(g * head, (g + 1) * head))
                        (odd_ref if j % 2 else even_ref)[at] = value_grad[src]
        dq, gain_grad = heads_backward(ungroup(pieces), qpre[...], qg[...], cos[...], sin[...])
        dq_out[...] = dq.astype(LOW)
        gain_out[...] = gain_grad

    lane_kv = shape_of((lanes * tokens, kv_width), LOW)
    k_odd, k_even, v_odd, v_even, dq_low, dg_low, branch_rows, grad_qgain = run_kernel(
        back_body,
        [
            lane_kv,
            lane_kv,
            lane_kv,
            lane_kv,
            shape_of((tokens, q_width), LOW),
            shape_of((tokens, q_width), LOW),
            shape_of((tokens, width), LOW),
            shape_of((1, head), F32),
        ],
        [
            query_low,
            query_pre,
            gate_pre,
            attended,
            cosine,
            sine,
            q_gain,
            query_pos,
            key_pos,
            *keys,
            *values,
            *w_o,
            branch_grad,
        ],
        5 * att_flops // 2 + 2 * tokens * width * q_width,
    )
    key_halves = join_lanes(k_even, k_odd)
    value_halves = join_lanes(v_even, v_odd)
    gates_last = last_steps(gates, 1, (key_halves, value_halves))
    ups_last = last_steps(ups, 0, (key_halves, value_halves))
    key_grad = scatter_lanes(key_halves, back_a, down_raw)
    value_grad = scatter_lanes(value_halves, back_b, down_raw)

    def write_lanes(value, odd_ref, even_ref, lane):
        for j in range(n):
            place = lane.index(j & ~1)
            at = slice(place * block, (place + 1) * block)
            (odd_ref if j % 2 else even_ref)[at] = value[j * block : (j + 1) * block].astype(LOW)

    lane_w = shape_of((lanes * block, q_width), LOW)

    def weight_body(normed_ref, dq, dg, bg, gated, *refs):
        wq, wg, outs = split_refs(refs, steps, steps)
        g_odd, g_even, o_odd, o_even, q_odd, q_even, acc = outs
        low = normed_ref[...]
        write_lanes(dot_tn(low, dg[...]), g_odd, g_even, lane_a)
        write_lanes(dot_tn(bg[...], gated[...]), o_odd, o_even, lane_b)
        write_lanes(dot_tn(low, dq[...]), q_odd, q_even, lane_a)
        acc[...] = dot_nt(dq[...], rows_of(wq, q_place)) + dot_nt(dg[...], rows_of(wg, g_place))

    g_odd, g_even, o_odd, o_even, q_odd, q_even, normed_acc = run_kernel(
        weight_body,
        [lane_w] * 6 + [shape_of((tokens, width), F32)],
        [after(normed, down_raw), dq_low, dg_low, branch_rows, gated_low, *w_q, *w_g],
        10 * tokens * width * q_width,
    )

    def key_body(dk, dv, kpre, cos, sin, kg, normed_ref, acc, *refs):
        wkv, (kv_odd, kv_even, gain_out, send_out) = split_refs(refs, steps)
        dkey, gain_grad = heads_backward(
            dk[...] * scale, kpre[...], kg[...], cos[...], sin[...]
        )
        gain_out[...] = gain_grad
        low = jnp.concatenate([dkey.astype(LOW), dv[...].astype(LOW)], axis=1)
        write_blocks(acc[...] + dot_nt(low, rows_of(wkv, kv_place)), send_out)
        write_lanes(dot_tn(normed_ref[...], low), kv_odd, kv_even, lane_b)

    lane_w2 = shape_of((lanes * block, 2 * kv_width), LOW)
    kv_odd, kv_even, grad_kgain, send = run_kernel(
        key_body,
        [lane_w2, lane_w2, shape_of((1, head), F32), block_out],
        [key_grad, value_grad, key_pre, cosine, sine, k_gain, normed, normed_acc, *w_kv],
        8 * tokens * width * kv_width,
    )
    gate_raw, grad_hgate = return_units(gates_last, down_raw)
    got = exchange_tp(after(send, gate_raw))
    _, grad_hup = return_units(ups_last, got)
    ready = (key_grad, value_grad)
    g_odd, o_odd, q_odd = after((g_odd, o_odd, q_odd), *ready)
    grad_gating = scatter_lanes(join_lanes(g_even, g_odd), back_a)
    grad_outproj = scatter_lanes(join_lanes(o_even, o_odd), back_b).T
    grad_query = scatter_lanes(join_lanes(q_even, q_odd), back_a, got)
    grad_kv = scatter_lanes(join_lanes(kv_even, kv_odd), back_b, got)

    def input_body(me_ref, x, gain, mg, got_ref, in_out, gain_out, total_ref):
        total_ref[...] = sum_blocks(got_ref)
        total = read_permuted(total_ref, me_ref)
        rows = x[...]
        r = inverse_rms(rows)
        unit = rows * r
        gain_out[...] = jnp.sum(total * unit, axis=0, keepdims=True)
        u = total * gain[...]
        in_out[...] = mg[...] + r * (u - unit * jnp.mean(u * unit, -1, keepdims=True))

    input_grad, grad_first = run_part(
        input_body,
        [part_f32, gain_f32],
        [x_part, first_gain[None], middle_grad, outer_permute(got)],
    )
    gains = jnp.concatenate([grad_first, grad_second, grad_qgain, grad_kgain], axis=1)
    gains = gains.reshape(-1, head)
    for mask in [1 << b for b in range((p - 1).bit_length())]:
        gains = gains + swap(gains, "tp", mask)
    for mask in masks:
        gains = gains + swap(gains, "seq", mask)
    gains = gains.reshape(-1)

    ffn_out = tree_sum([out_got[b].astype(F32) for b in range(p)])
    layer_rows = (middle + ffn_out).astype(LOW)

    grad_hgate = grad_hgate.T
    grad_hup = grad_hup.T
    return (
        layer_rows.reshape(micros, part, width),
        input_grad.reshape(micros, part, width),
        gains[:width],
        grad_query,
        grad_kv[:, :kv_width],
        grad_kv[:, kv_width:],
        grad_gating,
        grad_outproj,
        gains[2 * width : 2 * width + head],
        gains[2 * width + head :],
        gains[width : 2 * width],
        grad_hgate,
        grad_hup,
        grad_hdown,
    )


def solution(mesh):
    in_specs = (
        P(None, "seq", None),
        P(None, "seq"),
        P(),
        P("seq", "tp"),
        P("seq", "tp"),
        P("seq", "tp"),
        P("seq", "tp"),
        P("tp", "seq"),
        P(),
        P(),
        P(),
        P("tp", "seq"),
        P("tp", "seq"),
        P("seq", "tp"),
        P(None, ("seq", "tp"), None),
    )
    out_specs = (
        P(None, ("seq", "tp"), None),
        P(None, ("seq", "tp"), None),
        P(),
        P("seq", "tp"),
        P("seq", "tp"),
        P("seq", "tp"),
        P("seq", "tp"),
        P("tp", "seq"),
        P(),
        P(),
        P(),
        P("tp", "seq"),
        P("tp", "seq"),
        P("seq", "tp"),
    )
    return jax.shard_map(
        per_device, mesh=mesh, in_specs=in_specs, out_specs=out_specs, check_vma=False
    )
```

profile of v0, /device:TPU:0, one launch (start us, length us, event | category | flops | bytes accessed | tf_op | source)
XLA Modules:
  0.0 434.8 jit_solution(11019114067591438976)
XLA Ops:
  14.3 5.0 %all-to-all-start = ((bf16[4,3,192,512]{3,2,1,0:T(8,128)(2,1)}), bf16[4,3,192,512]{3,2,1,0:T(8,128)(2,1)S(1)}, u32[]{:S(2)}, u32[]{:S(2)}) async-start(bf16[4,3,192,512]{3,2,1,0:T(8,128)(2,1)} %copy.54), calls=%async_computation | async-start | bytes 4718592 | tf_op jit(solution)/shard_map/all_to_all | solution.py:109
  27.2 14.0 %collective-permute-done.1.refs_16_.refs_11_ = bf16[1,256,512]{2,1,0:T(8,128)(2,1)S(1)} collective-permute-done((bf16[1,256,512]{2,1,0:T(8,128)(2,1)S(1)}, bf16[1,256,512]{2,1,0:T(8,128)(2,1)S(1)}, u32[]{:S(2)}, u32[]{:S(2)}) %collective-permute-start.1) | collective-permute-done | bytes 262176 | tf_op jit(solution)/shard_map/ppermute | solution.py:57
  48.3 5.2 %shard_map.254 = (bf16[256,2048]{1,0:T(8,128)(2,1)}, f32[256,512]{1,0:T(8,128)}, f32[256,256]{1,0:T(8,128)}, bf16[256,512]{1,0:T(8,128)(2,1)}, bf16[256,256]{1,0:T(8,128)(2,1)}, /*index=5*/bf16[256,256]{1,0:T(8,128)(2,1)}) custom-call(s32[2]{0:T(128)} %pad_add_fusion.me_ref, bf16[256,2048]{1,0:T(8,128)(2,1)} %bitcast.129, f32[1,2048]{1,0:T(1,128)} %bitcast.159, ...), custom_call_target="tpu_custom_call" | custom-call | flops 134217728 | bytes 984192 | tf_op jit(solution)/shard_map/pallas_call | solution.py:27
  65.2 4.6 %collective-permute-done.15.refs_7_ = bf16[2,256,256]{2,1,0:T(8,128)(2,1)} collective-permute-done((bf16[2,256,256]{2,1,0:T(8,128)(2,1)S(1)}, bf16[2,256,256]{2,1,0:T(8,128)(2,1)}, u32[]{:S(2)}, u32[]{:S(2)}) %collective-permute-start.15) | collective-permute-done | bytes 262176 | tf_op jit(solution)/shard_map/ppermute | solution.py:57
  73.2 4.8 %all-to-all-start.1 = ((bf16[4,64,2048]{2,1,0:T(8,128)(2,1)}), bf16[4,64,2048]{2,1,0:T(8,128)(2,1)S(1)}, u32[]{:S(2)}, u32[]{:S(2)}) async-start(bf16[4,64,2048]{2,1,0:T(8,128)(2,1)} %broadcast_in_dim.59), calls=%async_computation.1 | async-start | bytes 2097152 | tf_op jit(solution)/shard_map/all_to_all | solution.py:109
  83.3 8.0 %shard_map.255 = (f32[256,512]{1,0:T(8,128)}, f32[256,512]{1,0:T(8,128)}, bf16[256,512]{1,0:T(8,128)(2,1)}, bf16[4,64,2048]{2,1,0:T(8,128)(2,1)}) custom-call(bf16[256,512]{1,0:T(8,128)(2,1)} %get-tuple-element.112.q, bf16[256,2048]{1,0:T(8,128)(2,1)} %get-tuple-element.156.normed_ref, s32[256,1]{1,0:T(8,128)} %copy.55.qpos, s32[1,1024]{1,0:T(1,128)} %bitcast.161, ...), custom_call_target="tpu_custom_call" | custom-call | flops 201326592 | bytes 1245824 | tf_op jit(solution)/shard_map/pallas_call | solution.py:27
  91.3 13.1 %all-to-all-done.1 = bf16[4,64,2048]{2,1,0:T(8,128)(2,1)S(1)} async-done(((bf16[4,64,2048]{2,1,0:T(8,128)(2,1)}), bf16[4,64,2048]{2,1,0:T(8,128)(2,1)S(1)}, u32[]{:S(2)}, u32[]{:S(2)}) %all-to-all-start.1) | async-done | bytes 1048608 | tf_op jit(solution)/shard_map/all_to_all | solution.py:109
  104.4 4.2 all-to-all-start.2
  117.3 17.0 %all-to-all-done.2.got_ref = bf16[4,64,2048]{2,1,0:T(8,128)(2,1)} async-done(((bf16[4,64,2048]{2,1,0:T(8,128)(2,1)}), bf16[4,64,2048]{2,1,0:T(8,128)(2,1)}, u32[]{:S(2)}, u32[]{:S(2)}) %all-to-all-start.2) | async-done | bytes 1048608 | tf_op jit(solution)/shard_map/all_to_all | solution.py:109
  137.1 14.5 %all-to-all-start.3 = ((bf16[4,64,2048]{2,1,0:T(8,128)(2,1)}), bf16[4,64,2048]{2,1,0:T(8,128)(2,1)S(1)}, u32[]{:S(2)}, u32[]{:S(2)}) async-start(bf16[4,64,2048]{2,1,0:T(8,128)(2,1)} %get-tuple-element.120), calls=%async_computation.3 | async-start | bytes 2097152 | tf_op jit(solution)/shard_map/all_to_all | solution.py:109
  152.2 12.2 %collective-permute-done.30.r_6_.r_10_ = bf16[2,3,96,2048]{3,2,1,0:T(8,128)(2,1)} collective-permute-done((bf16[2,3,96,2048]{3,2,1,0:T(8,128)(2,1)}, bf16[2,3,96,2048]{3,2,1,0:T(8,128)(2,1)}, u32[]{:S(2)}, u32[]{:S(2)}) %collective-permute-start.30) | collective-permute-done | bytes 2359328 | tf_op jit(solution)/shard_map/ppermute | solution.py:57
  164.4 12.2 %all-to-all-done.3 = bf16[4,64,2048]{2,1,0:T(8,128)(2,1)S(1)} async-done(((bf16[4,64,2048]{2,1,0:T(8,128)(2,1)}), bf16[4,64,2048]{2,1,0:T(8,128)(2,1)S(1)}, u32[]{:S(2)}, u32[]{:S(2)}) %all-to-all-start.3) | async-done | bytes 1048608 | tf_op jit(solution)/shard_map/all_to_all | solution.py:109
  177.6 8.2 %shard_map.257 = (f32[768,256]{1,0:T(8,128)}, f32[768,256]{1,0:T(8,128)}, bf16[768,256]{1,0:T(8,128)(2,1)}, f32[256,2048]{1,0:T(8,128)}) custom-call(bf16[256,2048]{1,0:T(8,128)(2,1)} %bitcast.107, bf16[1,3,96,2048]{3,2,1,0:T(8,128)(2,1)} %copy-done.2, bf16[1,3,96,2048]{3,2,1,0:T(8,128)(2,1)} %collective-permute-done.24.r_2_.r_6_, ...), custom_call_target="tpu_custom_call" | custom-call | flops 301989888 | bytes 1441792 | tf_op jit(solution)/shard_map/pallas_call | solution.py:452
  187.2 8.5 %shard_map.258 = (f32[768,256]{1,0:T(8,128)}, f32[768,256]{1,0:T(8,128)}, bf16[768,256]{1,0:T(8,128)(2,1)}, bf16[256,2048]{1,0:T(8,128)(2,1)}) custom-call(bf16[256,2048]{1,0:T(8,128)(2,1)} %bitcast.108, bf16[2,3,96,2048]{3,2,1,0:T(8,128)(2,1)} %collective-permute-done.25.r_1_.r_5_, bf16[2,3,96,2048]{3,2,1,0:T(8,128)(2,1)} %collective-permute-done.27.r_2_.r_6_, ...), custom_call_target="tpu_custom_call" | custom-call | flops 301989888 | bytes 1441792 | tf_op jit(solution)/shard_map/pallas_call | solution.py:452
  195.7 3.5 all-to-all-start.4
  199.2 12.0 %shard_map.259 = (bf16[384,2048]{1,0:T(8,128)(2,1)}, bf16[384,2048]{1,0:T(8,128)(2,1)}, bf16[384,2048]{1,0:T(8,128)(2,1)}, bf16[384,2048]{1,0:T(8,128)(2,1)}, bf...) custom-call(bf16[256,2048]{1,0:T(8,128)(2,1)} %bitcast.109, bf16[256,2048]{1,0:T(8,128)(2,1)} %bitcast.113, ...), custom_call_target="tpu_custom_call" | custom-call | flops 603979776 | bytes 2883584 | tf_op jit(solution)/shard_map/pallas_call | solution.py:526
  212.4 12.3 %shard_map.260 = (bf16[384,2048]{1,0:T(8,128)(2,1)}, bf16[384,2048]{1,0:T(8,128)(2,1)}, bf16[384,2048]{1,0:T(8,128)(2,1)}, bf16[384,2048]{1,0:T(8,128)(2,1)}, bf...) custom-call(bf16[256,2048]{1,0:T(8,128)(2,1)} %bitcast.110, ...), custom_call_target="tpu_custom_call" | custom-call | flops 603979776 | bytes 2883584 | tf_op jit(solution)/shard_map/pallas_call | solution.py:526
  225.0 5.2 %all-to-all-start.5 = ((bf16[4,64,2048]{2,1,0:T(8,128)(2,1)}), bf16[4,64,2048]{2,1,0:T(8,128)(2,1)S(1)}, u32[]{:S(2)}, u32[]{:S(2)}) async-start(bf16[4,64,2048]{2,1,0:T(8,128)(2,1)} %bitcast.150), calls=%async_computation.5 | async-start | bytes 2097152 | tf_op jit(solution)/shard_map/all_to_all | solution.py:109
  236.3 3.3 add_convert_fusion.6
  244.4 3.3 add_convert_fusion.2
  262.9 5.0 %all-to-all-start.6 = ((bf16[4,64,2048]{2,1,0:T(8,128)(2,1)}), bf16[4,64,2048]{2,1,0:T(8,128)(2,1)S(1)}, u32[]{:S(2)}, u32[]{:S(2)}) async-start(bf16[4,64,2048]{2,1,0:T(8,128)(2,1)} %get-tuple-element.141), calls=%async_computation.6 | async-start | bytes 2097152 | tf_op jit(solution)/shard_map/all_to_all | solution.py:109
  268.7 12.0 %collective-permute-done.36 = bf16[96,2048]{1,0:T(8,128)(2,1)} collective-permute-done((bf16[96,2048]{1,0:T(8,128)(2,1)}, bf16[96,2048]{1,0:T(8,128)(2,1)}, u32[]{:S(2)}, u32[]{:S(2)}) %collective-permute-start.36) | collective-permute-done | bytes 393248 | tf_op jit(solution)/shard_map/ppermute | solution.py:57
  293.1 9.4 %shard_map.262 = (bf16[1024,256]{1,0:T(8,128)(2,1)}, bf16[1024,256]{1,0:T(8,128)(2,1)}, bf16[1024,256]{1,0:T(8,128)(2,1)}, bf16[1024,256]{1,0:T(8,128)(2,1)}, bf...) custom-call(bf16[256,512]{1,0:T(8,128)(2,1)} %get-tuple-element.112.q, ...), custom_call_target="tpu_custom_call" | custom-call | flops 234881024 | bytes 1377024 | tf_op jit(solution)/shard_map/pallas_call | solution.py:27
  306.0 4.5 %all-to-all-start.7 = ((bf16[4,192,512]{2,1,0:T(8,128)(2,1)}), bf16[4,192,512]{2,1,0:T(8,128)(2,1)}, u32[]{:S(2)}, u32[]{:S(2)}) async-start(bf16[4,192,512]{2,1,0:T(8,128)(2,1)} %maximum_bitcast_fusion.1), calls=%async_computation.7 | async-start | bytes 1572864 | tf_op jit(solution)/shard_map/all_to_all | solution.py:109
  326.3 3.9 collective-permute-done.69
  331.2 4.5 %all-to-all-start.8 = ((bf16[4,192,512]{2,1,0:T(8,128)(2,1)}), bf16[4,192,512]{2,1,0:T(8,128)(2,1)S(1)}, u32[]{:S(2)}, u32[]{:S(2)}) async-start(bf16[4,192,512]{2,1,0:T(8,128)(2,1)} %maximum_bitcast_fusion.2), calls=%async_computation.8 | async-start | bytes 1572864 | tf_op jit(solution)/shard_map/all_to_all | solution.py:109
  338.4 7.3 %shard_map.263 = (bf16[1024,512]{1,0:T(8,128)(2,1)}, bf16[1024,512]{1,0:T(8,128)(2,1)}, bf16[1024,512]{1,0:T(8,128)(2,1)}, bf16[1024,512]{1,0:T(8,128)(2,1)}, bf...) custom-call(bf16[256,2048]{1,0:T(8,128)(2,1)} %get-tuple-element.156.normed_ref, ...), custom_call_target="tpu_custom_call" | custom-call | flops 335544320 | bytes 1933312 | tf_op jit(solution)/shard_map/pallas_call | solution.py:27
  349.9 5.9 %shard_map.264 = (bf16[1024,512]{1,0:T(8,128)(2,1)}, bf16[1024,512]{1,0:T(8,128)(2,1)}, f32[1,128]{1,0:T(1,128)}, bf16[4,64,2048]{2,1,0:T(8,128)(2,1)}) custom-call(f32[256,256]{1,0:T(8,128)} %convert_add_fusion.4.dk, f32[256,256]{1,0:T(8,128)} %convert_add_fusion.3.dv, f32[256,256]{1,0:T(8,128)} %get-tuple-element.155.kpre, ...), custom_call_target="tpu_custom_call" | custom-call | flops 134217728 | bytes 1179776 | tf_op jit(solution)/shard_map/pallas_call | solution.py:27
  361.0 5.2 %all-to-all-start.9 = ((bf16[4,64,2048]{2,1,0:T(8,128)(2,1)}), bf16[4,64,2048]{2,1,0:T(8,128)(2,1)S(1)}, u32[]{:S(2)}, u32[]{:S(2)}) async-start(bf16[4,64,2048]{2,1,0:T(8,128)(2,1)} %get-tuple-element.172), calls=%async_computation.9 | async-start | bytes 2097152 | tf_op jit(solution)/shard_map/all_to_all | solution.py:109
  386.0 6.1 %all-to-all-done.9.got_ref = bf16[4,64,2048]{2,1,0:T(8,128)(2,1)S(1)} async-done(((bf16[4,64,2048]{2,1,0:T(8,128)(2,1)}), bf16[4,64,2048]{2,1,0:T(8,128)(2,1)S(1)}, u32[]{:S(2)}, u32[]{:S(2)}) %all-to-all-start.9) | async-done | bytes 1048608 | tf_op jit(solution)/shard_map/all_to_all | solution.py:109
  408.2 3.8 all-to-all-start.10
  427.3 5.5 %all-to-all-done.10 = bf16[4,192,512]{2,1,0:T(8,128)(2,1)S(1)} async-done(((bf16[4,192,512]{2,1,0:T(8,128)(2,1)}), bf16[4,192,512]{2,1,0:T(8,128)(2,1)S(1)}, u32[]{:S(2)}, u32[]{:S(2)}) %all-to-all-start.10) | async-done | bytes 786464 | tf_op jit(solution)/shard_map/all_to_all | solution.py:109
  (368 shorter events, 188.9 us)
Async XLA Ops:
  14.3 57.8 %all-to-all-start = ((bf16[4,3,192,512]{3,2,1,0:T(8,128)(2,1)}), bf16[4,3,192,512]{3,2,1,0:T(8,128)(2,1)S(1)}, u32[]{:S(2)}, u32[]{:S(2)}) async-start(bf16[4,3,192,512]{3,2,1,0:T(8,128)(2,1)} %copy.54), calls=%async_computation | async-start | bytes 4718592 | tf_op jit(solution)/shard_map/all_to_all | solution.py:109
  73.2 31.2 %all-to-all-start.1 = ((bf16[4,64,2048]{2,1,0:T(8,128)(2,1)}), bf16[4,64,2048]{2,1,0:T(8,128)(2,1)S(1)}, u32[]{:S(2)}, u32[]{:S(2)}) async-start(bf16[4,64,2048]{2,1,0:T(8,128)(2,1)} %broadcast_in_dim.59), calls=%async_computation.1 | async-start | bytes 2097152 | tf_op jit(solution)/shard_map/all_to_all | solution.py:109
  78.6 30.0 %collective-permute-start.28 = (bf16[1,3,96,2048]{3,2,1,0:T(8,128)(2,1)S(1)}, bf16[1,3,96,2048]{3,2,1,0:T(8,128)(2,1)}, u32[]{:S(2)}, u32[]{:S(2)}) collective-permute-start(bf16[1,3,96,2048]{3,2,1,0:T(8,128)(2,1)S(1)} %get-tuple-element.262.r_4_.r_8_), channel_id=1, source_target_pairs={{0,16},{4,20},{8,24},{12,28},{16,0},{20,4},{24,8},{28,12},{1,17},{... | collective-permute-start | bytes 3538952 | tf_op jit(solution)/shard_map/ppermute | solution.py:57
  79.2 32.9 %collective-permute-start.24 = (bf16[1,3,96,2048]{3,2,1,0:T(8,128)(2,1)S(1)}, bf16[1,3,96,2048]{3,2,1,0:T(8,128)(2,1)}, u32[]{:S(2)}, u32[]{:S(2)}) collective-permute-start(bf16[1,3,96,2048]{3,2,1,0:T(8,128)(2,1)S(1)} %get-tuple-element.263.r_1_.r_5_), channel_id=1, source_target_pairs={{0,8},{4,12},{8,0},{12,4},{16,24},{20,28},{24,16},{28,20},{1,9},{5... | collective-permute-start | bytes 3538952 | tf_op jit(solution)/shard_map/ppermute | solution.py:57
  104.4 29.8 %all-to-all-start.2 = ((bf16[4,64,2048]{2,1,0:T(8,128)(2,1)}), bf16[4,64,2048]{2,1,0:T(8,128)(2,1)}, u32[]{:S(2)}, u32[]{:S(2)}) async-start(bf16[4,64,2048]{2,1,0:T(8,128)(2,1)} %get-tuple-element.118), calls=%async_computation.2 | async-start | bytes 2097152 | tf_op jit(solution)/shard_map/all_to_all | solution.py:109
  111.6 52.8 %collective-permute-start.30 = (bf16[2,3,96,2048]{3,2,1,0:T(8,128)(2,1)}, bf16[2,3,96,2048]{3,2,1,0:T(8,128)(2,1)}, u32[]{:S(2)}, u32[]{:S(2)}) collective-permute-start(bf16[2,3,96,2048]{3,2,1,0:T(8,128)(2,1)} %pad_maximum_fusion.1), channel_id=1, source_target_pairs={{0,8},{4,12},{8,0},{12,4},{16,24},{20,28},{24,16},{28,20},{1,9},{5... | collective-permute-start | bytes 7077896 | tf_op jit(solution)/shard_map/ppermute | solution.py:57
  115.0 61.7 %collective-permute-start.26 = (bf16[2,3,96,2048]{3,2,1,0:T(8,128)(2,1)}, bf16[2,3,96,2048]{3,2,1,0:T(8,128)(2,1)}, u32[]{:S(2)}, u32[]{:S(2)}) collective-permute-start(bf16[2,3,96,2048]{3,2,1,0:T(8,128)(2,1)} %pad_maximum_fusion), channel_id=1, source_target_pairs={{0,16},{4,20},{8,24},{12,28},{16,0},{20,4},{24,8},{28,12},{1,17},{... | collective-permute-start | bytes 7077896 | tf_op jit(solution)/shard_map/ppermute | solution.py:57
  137.1 39.5 %all-to-all-start.3 = ((bf16[4,64,2048]{2,1,0:T(8,128)(2,1)}), bf16[4,64,2048]{2,1,0:T(8,128)(2,1)S(1)}, u32[]{:S(2)}, u32[]{:S(2)}) async-start(bf16[4,64,2048]{2,1,0:T(8,128)(2,1)} %get-tuple-element.120), calls=%async_computation.3 | async-start | bytes 2097152 | tf_op jit(solution)/shard_map/all_to_all | solution.py:109
  151.6 34.1 %collective-permute-start.29 = (bf16[2,3,96,2048]{3,2,1,0:T(8,128)(2,1)}, bf16[2,3,96,2048]{3,2,1,0:T(8,128)(2,1)S(1)}, u32[]{:S(2)}, u32[]{:S(2)}) collective-permute-start(bf16[2,3,96,2048]{3,2,1,0:T(8,128)(2,1)} %pad_maximum_fusion.1), channel_id=1, source_target_pairs={{0,4},{4,0},{8,12},{12,8},{16,20},{20,16},{24,28},{28,24},{1,5},{5... | collective-permute-start | bytes 7077896 | tf_op jit(solution)/shard_map/ppermute | solution.py:57
  151.7 34.1 %collective-permute-start.25 = (bf16[2,3,96,2048]{3,2,1,0:T(8,128)(2,1)}, bf16[2,3,96,2048]{3,2,1,0:T(8,128)(2,1)}, u32[]{:S(2)}, u32[]{:S(2)}) collective-permute-start(bf16[2,3,96,2048]{3,2,1,0:T(8,128)(2,1)} %pad_maximum_fusion), channel_id=1, source_target_pairs={{0,4},{4,0},{8,12},{12,8},{16,20},{20,16},{24,28},{28,24},{1,5},{5... | collective-permute-start | bytes 7077896 | tf_op jit(solution)/shard_map/ppermute | solution.py:57
  195.7 29.3 %all-to-all-start.4 = ((bf16[4,64,2048]{2,1,0:T(8,128)(2,1)}), bf16[4,64,2048]{2,1,0:T(8,128)(2,1)S(1)}, u32[]{:S(2)}, u32[]{:S(2)}) async-start(bf16[4,64,2048]{2,1,0:T(8,128)(2,1)} %bitcast.151), calls=%async_computation.4 | async-start | bytes 2097152 | tf_op jit(solution)/shard_map/all_to_all | solution.py:109
  211.8 23.9 %collective-permute-start.44 = (bf16[384,2048]{1,0:T(8,128)(2,1)}, bf16[384,2048]{1,0:T(8,128)(2,1)}, u32[]{:S(2)}, u32[]{:S(2)}) collective-permute-start(bf16[384,2048]{1,0:T(8,128)(2,1)} %get-tuple-element.164), channel_id=1, source_target_pairs={{0,4},{4,0},{8,12},{12,8},{16,20},{20,16},{24,28},{28,24},{1,5},{5... | collective-permute-start | bytes 4718600 | tf_op jit(solution)/shard_map/ppermute | solution.py:57
  211.9 31.0 %collective-permute-start.67 = (bf16[384,2048]{1,0:T(8,128)(2,1)}, bf16[384,2048]{1,0:T(8,128)(2,1)}, u32[]{:S(2)}, u32[]{:S(2)}) collective-permute-start(bf16[384,2048]{1,0:T(8,128)(2,1)} %get-tuple-element.192), channel_id=1, source_target_pairs={{0,4},{4,0},{8,12},{12,8},{16,20},{20,16},{24,28},{28,24},{1,5},{5... | collective-permute-start | bytes 4718600 | tf_op jit(solution)/shard_map/ppermute | solution.py:57
  212.3 35.4 %collective-permute-start.70 = (bf16[384,2048]{1,0:T(8,128)(2,1)}, bf16[384,2048]{1,0:T(8,128)(2,1)}, u32[]{:S(2)}, u32[]{:S(2)}) collective-permute-start(bf16[384,2048]{1,0:T(8,128)(2,1)} %get-tuple-element.198), channel_id=1, source_target_pairs={{0,4},{4,0},{8,12},{12,8},{16,20},{20,16},{24,28},{28,24},{1,5},{5... | collective-permute-start | bytes 4718600 | tf_op jit(solution)/shard_map/ppermute | solution.py:57
  225.0 33.8 %all-to-all-start.5 = ((bf16[4,64,2048]{2,1,0:T(8,128)(2,1)}), bf16[4,64,2048]{2,1,0:T(8,128)(2,1)S(1)}, u32[]{:S(2)}, u32[]{:S(2)}) async-start(bf16[4,64,2048]{2,1,0:T(8,128)(2,1)} %bitcast.150), calls=%async_computation.5 | async-start | bytes 2097152 | tf_op jit(solution)/shard_map/all_to_all | solution.py:109
  239.6 46.3 %collective-permute-start.45 = (bf16[192,2048]{1,0:T(8,128)(2,1)}, bf16[192,2048]{1,0:T(8,128)(2,1)}, u32[]{:S(2)}, u32[]{:S(2)}) collective-permute-start(bf16[192,2048]{1,0:T(8,128)(2,1)} %get-tuple-element.254), channel_id=1, source_target_pairs={{0,8},{4,12},{8,0},{12,4},{16,24},{20,28},{24,16},{28,20},{1,9},{5... | collective-permute-start | bytes 2359304 | tf_op jit(solution)/shard_map/ppermute | solution.py:57
  242.9 46.4 %collective-permute-start.48 = (bf16[192,2048]{1,0:T(8,128)(2,1)}, bf16[192,2048]{1,0:T(8,128)(2,1)}, u32[]{:S(2)}, u32[]{:S(2)}) collective-permute-start(bf16[192,2048]{1,0:T(8,128)(2,1)} %get-tuple-element.256), channel_id=1, source_target_pairs={{0,16},{4,20},{8,24},{12,28},{16,0},{20,4},{24,8},{28,12},{1,17},{... | collective-permute-start | bytes 2359304 | tf_op jit(solution)/shard_map/ppermute | solution.py:57
  254.6 26.2 %collective-permute-start.36 = (bf16[96,2048]{1,0:T(8,128)(2,1)}, bf16[96,2048]{1,0:T(8,128)(2,1)}, u32[]{:S(2)}, u32[]{:S(2)}) collective-permute-start(bf16[96,2048]{1,0:T(8,128)(2,1)} %add_convert_fusion.36), channel_id=1, source_target_pairs={{0,16},{4,20},{8,24},{12,28},{16,0},{20,4},{24,8},{28,12},{1,17},{... | collective-permute-start | bytes 1179656 | tf_op jit(solution)/shard_map/ppermute | solution.py:57
  257.2 23.5 %collective-permute-start.39 = (bf16[96,2048]{1,0:T(8,128)(2,1)}, bf16[96,2048]{1,0:T(8,128)(2,1)}, u32[]{:S(2)}, u32[]{:S(2)}) collective-permute-start(bf16[96,2048]{1,0:T(8,128)(2,1)} %add_convert_fusion.33), channel_id=1, source_target_pairs={{0,8},{4,12},{8,0},{12,4},{16,24},{20,28},{24,16},{28,20},{1,9},{5... | collective-permute-start | bytes 1179656 | tf_op jit(solution)/shard_map/ppermute | solution.py:57
  262.9 29.3 %all-to-all-start.6 = ((bf16[4,64,2048]{2,1,0:T(8,128)(2,1)}), bf16[4,64,2048]{2,1,0:T(8,128)(2,1)S(1)}, u32[]{:S(2)}, u32[]{:S(2)}) async-start(bf16[4,64,2048]{2,1,0:T(8,128)(2,1)} %get-tuple-element.141), calls=%async_computation.6 | async-start | bytes 2097152 | tf_op jit(solution)/shard_map/all_to_all | solution.py:109
  283.9 31.7 %collective-permute-start.68 = (bf16[192,2048]{1,0:T(8,128)(2,1)}, bf16[192,2048]{1,0:T(8,128)(2,1)}, u32[]{:S(2)}, u32[]{:S(2)}) collective-permute-start(bf16[192,2048]{1,0:T(8,128)(2,1)} %get-tuple-element.194), channel_id=1, source_target_pairs={{0,8},{4,12},{8,0},{12,4},{16,24},{20,28},{24,16},{28,20},{1,9},{5... | collective-permute-start | bytes 2359304 | tf_op jit(solution)/shard_map/ppermute | solution.py:57
  285.4 32.7 %collective-permute-start.71 = (bf16[192,2048]{1,0:T(8,128)(2,1)}, bf16[192,2048]{1,0:T(8,128)(2,1)}, u32[]{:S(2)}, u32[]{:S(2)}) collective-permute-start(bf16[192,2048]{1,0:T(8,128)(2,1)} %get-tuple-element.200), channel_id=1, source_target_pairs={{0,16},{4,20},{8,24},{12,28},{16,0},{20,4},{24,8},{28,12},{1,17},{... | collective-permute-start | bytes 2359304 | tf_op jit(solution)/shard_map/ppermute | solution.py:57
  287.8 33.7 %collective-permute-start.46 = (bf16[96,2048]{1,0:T(8,128)(2,1)}, bf16[96,2048]{1,0:T(8,128)(2,1)}, u32[]{:S(2)}, u32[]{:S(2)}) collective-permute-start(bf16[96,2048]{1,0:T(8,128)(2,1)} %add_convert_fusion.30), channel_id=1, source_target_pairs={{0,16},{4,20},{8,24},{12,28},{16,0},{20,4},{24,8},{28,12},{1,17},{... | collective-permute-start | bytes 1179656 | tf_op jit(solution)/shard_map/ppermute | solution.py:57
  306.0 25.2 %all-to-all-start.7 = ((bf16[4,192,512]{2,1,0:T(8,128)(2,1)}), bf16[4,192,512]{2,1,0:T(8,128)(2,1)}, u32[]{:S(2)}, u32[]{:S(2)}) async-start(bf16[4,192,512]{2,1,0:T(8,128)(2,1)} %maximum_bitcast_fusion.1), calls=%async_computation.7 | async-start | bytes 1572864 | tf_op jit(solution)/shard_map/all_to_all | solution.py:109
  313.3 22.5 %collective-permute-start.42 = (bf16[512,256]{1,0:T(8,128)(2,1)}, bf16[512,256]{1,0:T(8,128)(2,1)S(1)}, u32[]{:S(2)}, u32[]{:S(2)}) collective-permute-start(bf16[512,256]{1,0:T(8,128)(2,1)} %get-tuple-element.272), channel_id=1, source_target_pairs={{0,16},{4,20},{8,24},{12,28},{16,0},{20,4},{24,8},{28,12},{1,17},{... | collective-permute-start | bytes 786440 | tf_op jit(solution)/shard_map/ppermute | solution.py:57
  321.5 27.8 %collective-permute-start.72 = (bf16[96,2048]{1,0:T(8,128)(2,1)}, bf16[96,2048]{1,0:T(8,128)(2,1)S(1)}, u32[]{:S(2)}, u32[]{:S(2)}) collective-permute-start(bf16[96,2048]{1,0:T(8,128)(2,1)} %add_convert_fusion.21), channel_id=1, source_target_pairs={{0,8},{4,12},{8,0},{12,4},{16,24},{20,28},{24,16},{28,20},{1,9},{5... | collective-permute-start | bytes 1179656 | tf_op jit(solution)/shard_map/ppermute | solution.py:57
  331.2 29.7 %all-to-all-start.8 = ((bf16[4,192,512]{2,1,0:T(8,128)(2,1)}), bf16[4,192,512]{2,1,0:T(8,128)(2,1)S(1)}, u32[]{:S(2)}, u32[]{:S(2)}) async-start(bf16[4,192,512]{2,1,0:T(8,128)(2,1)} %maximum_bitcast_fusion.2), calls=%async_computation.8 | async-start | bytes 1572864 | tf_op jit(solution)/shard_map/all_to_all | solution.py:109
  361.0 31.1 %all-to-all-start.9 = ((bf16[4,64,2048]{2,1,0:T(8,128)(2,1)}), bf16[4,64,2048]{2,1,0:T(8,128)(2,1)S(1)}, u32[]{:S(2)}, u32[]{:S(2)}) async-start(bf16[4,64,2048]{2,1,0:T(8,128)(2,1)} %get-tuple-element.172), calls=%async_computation.9 | async-start | bytes 2097152 | tf_op jit(solution)/shard_map/all_to_all | solution.py:109
  372.8 24.0 %collective-permute-start.62 = (bf16[512,512]{1,0:T(8,128)(2,1)}, bf16[512,512]{1,0:T(8,128)(2,1)}, u32[]{:S(2)}, u32[]{:S(2)}) collective-permute-start(bf16[512,512]{1,0:T(8,128)(2,1)} %get-tuple-element.267), channel_id=1, source_target_pairs={{0,8},{4,12},{8,0},{12,4},{16,24},{20,28},{24,16},{28,20},{1,9},{5... | collective-permute-start | bytes 1572872 | tf_op jit(solution)/shard_map/ppermute | solution.py:57
  376.2 35.8 %collective-permute-start.59 = (bf16[512,512]{1,0:T(8,128)(2,1)}, bf16[512,512]{1,0:T(8,128)(2,1)}, u32[]{:S(2)}, u32[]{:S(2)}) collective-permute-start(bf16[512,512]{1,0:T(8,128)(2,1)} %get-tuple-element.268), channel_id=1, source_target_pairs={{0,16},{4,20},{8,24},{12,28},{16,0},{20,4},{24,8},{28,12},{1,17},{... | collective-permute-start | bytes 1572872 | tf_op jit(solution)/shard_map/ppermute | solution.py:57
  379.3 35.9 %collective-permute-start.56 = (bf16[512,512]{1,0:T(8,128)(2,1)}, bf16[512,512]{1,0:T(8,128)(2,1)}, u32[]{:S(2)}, u32[]{:S(2)}) collective-permute-start(bf16[512,512]{1,0:T(8,128)(2,1)} %get-tuple-element.270), channel_id=1, source_target_pairs={{0,8},{4,12},{8,0},{12,4},{16,24},{20,28},{24,16},{28,20},{1,9},{5... | collective-permute-start | bytes 1572872 | tf_op jit(solution)/shard_map/ppermute | solution.py:57
  408.2 24.6 %all-to-all-start.10 = ((bf16[4,192,512]{2,1,0:T(8,128)(2,1)}), bf16[4,192,512]{2,1,0:T(8,128)(2,1)S(1)}, u32[]{:S(2)}, u32[]{:S(2)}) async-start(bf16[4,192,512]{2,1,0:T(8,128)(2,1)} %maximum_bitcast_fusion.3), calls=%async_computation.10 | async-start | bytes 1572864 | tf_op jit(solution)/shard_map/all_to_all | solution.py:109
  (114 other events, 1121.1 us)
where the time goes:
time: 441 us; the launch traced here: 435 us
  waiting for transfers between devices  130 us (29%)
  starting transfers between devices  111 us (25%)
  Pallas kernels  85.9 us (19%)
  other arithmetic  84.2 us (19%)
  local copies, waits for them, and re-layouts  22.1 us (5%)
    ppermute x73, waiting for transfers between devices, swap(): return lax.ppermute(value, axis, [(i, i ^ mask) for i in range(count)])  72.1 us
    all_to_all x11, starting transfers between devices, exchange_tp(): return lax.all_to_all(blocks, 'tp', 0, 0, tiled=True)  60.3 us
    all_to_all x11, waiting for transfers between devices, exchange_tp(): return lax.all_to_all(blocks, 'tp', 0, 0, tiled=True)  58 us
    ppermute x73, starting transfers between devices, swap(): return lax.ppermute(value, axis, [(i, i ^ mask) for i in range(count)])  50.5 us
    convert_element_type x24, other arithmetic, sum_halves(): (keep[at].astype(F32) + got[at].astype(F32)).astype(LOW)  43.4 us
    pallas_call x5, Pallas kernels, run_kernel(): pl.pallas_call(body, out_shape=outs, in_specs=specs, out_specs=[pl.BlockS...  35.9 us
    pallas_call x2, Pallas kernels, run_backward(): pl.pallas_call(lambda *r: backward_body(first, slots, len(held) // 2, *r)...  24.3 us
    pallas_call x2, Pallas kernels, run_forward(): pl.pallas_call(lambda *r: forward_body(last, slots, len(held) // 2, *r),...  16.7 us
  transfers between devices with their start and end apart: 84, of which 33 were waited for; matrix products, arithmetic and copies ran while one was open for 22% of the time, Pallas kernels for 18%

commit v1 on v0

--- a/solution.py
+++ b/solution.py
@@ -715,7 +715,7 @@
     ready = (key_grad, value_grad)
     g_odd, o_odd, q_odd = after((g_odd, o_odd, q_odd), *ready)
     grad_gating = scatter_lanes(join_lanes(g_even, g_odd), back_a)
-    grad_outproj = scatter_lanes(join_lanes(o_even, o_odd), back_b).T
+    grad_outproj = scatter_lanes(join_lanes(o_even, o_odd), back_b, got).T
     grad_query = scatter_lanes(join_lanes(q_even, q_odd), back_a, got)
     grad_kv = scatter_lanes(join_lanes(kv_even, kv_odd), back_b, got)
 

time: 441 us -> 437 us (level)
    all_to_all x11, waiting for transfers between devices: 58 us -> 49.1 us  [exchange_tp(): return lax.all_to_all(blocks, 'tp', 0, 0, tiled=True)]
    ppermute x73, waiting for transfers between devices: 72.1 us -> 79.7 us  [swap(): return lax.ppermute(value, axis, [(i, i ^ mask) for i in range(count)])]
    unnamed x130 -> x134, local copies, waits for them, and re-layouts: 15 us -> 16 us
  transfers between devices with their start and end apart: 84 -> 84, of which waited for: 33 -> 30; matrix products, arithmetic and copies ran while one was open for 22% -> 22% of each run, Pallas kernels for 18% -> 18%
where the time goes in v1:
time: 437 us; the launch traced here: 431 us
  waiting for transfers between devices  129 us (30%)
  starting transfers between devices  110 us (25%)
  Pallas kernels  85.9 us (20%)
  other arithmetic  82 us (19%)
  local copies, waits for them, and re-layouts  23 us (5%)
    ppermute x73, waiting for transfers between devices, swap(): return lax.ppermute(value, axis, [(i, i ^ mask) for i in range(count)])  79.7 us
    all_to_all x11, starting transfers between devices, exchange_tp(): return lax.all_to_all(blocks, 'tp', 0, 0, tiled=True)  60.6 us
    all_to_all x11, waiting for transfers between devices, exchange_tp(): return lax.all_to_all(blocks, 'tp', 0, 0, tiled=True)  49.1 us
    ppermute x73, starting transfers between devices, swap(): return lax.ppermute(value, axis, [(i, i ^ mask) for i in range(count)])  49 us
    convert_element_type x24, other arithmetic, sum_halves(): (keep[at].astype(F32) + got[at].astype(F32)).astype(LOW)  40.9 us
    pallas_call x5, Pallas kernels, run_kernel(): pl.pallas_call(body, out_shape=outs, in_specs=specs, out_specs=[pl.BlockS...  35.9 us
    pallas_call x2, Pallas kernels, run_backward(): pl.pallas_call(lambda *r: backward_body(first, slots, len(held) // 2, *r)...  24.3 us
    pallas_call x2, Pallas kernels, run_forward(): pl.pallas_call(lambda *r: forward_body(last, slots, len(held) // 2, *r),...  16.7 us
  transfers between devices with their start and end apart: 84, of which 30 were waited for; matrix products, arithmetic and copies ran while one was open for 22% of the time, Pallas kernels for 18%

profile of v1, /device:TPU:0, one launch (start us, length us, event | category | flops | bytes accessed | tf_op | source)
XLA Modules:
  0.0 431.0 jit_solution(12255962994699254244)
XLA Ops:
  14.3 5.0 %all-to-all-start = ((bf16[4,3,192,512]{3,2,1,0:T(8,128)(2,1)}), bf16[4,3,192,512]{3,2,1,0:T(8,128)(2,1)S(1)}, u32[]{:S(2)}, u32[]{:S(2)}) async-start(bf16[4,3,192,512]{3,2,1,0:T(8,128)(2,1)} %copy.54), calls=%async_computation | async-start | bytes 4718592 | tf_op jit(solution)/shard_map/all_to_all | solution.py:109
  27.2 14.0 %collective-permute-done.1.refs_16_.refs_11_ = bf16[1,256,512]{2,1,0:T(8,128)(2,1)S(1)} collective-permute-done((bf16[1,256,512]{2,1,0:T(8,128)(2,1)S(1)}, bf16[1,256,512]{2,1,0:T(8,128)(2,1)S(1)}, u32[]{:S(2)}, u32[]{:S(2)}) %collective-permute-start.1) | collective-permute-done | bytes 262176 | tf_op jit(solution)/shard_map/ppermute | solution.py:57
  48.3 5.3 %shard_map.254 = (bf16[256,2048]{1,0:T(8,128)(2,1)}, f32[256,512]{1,0:T(8,128)}, f32[256,256]{1,0:T(8,128)}, bf16[256,512]{1,0:T(8,128)(2,1)}, bf16[256,256]{1,0:T(8,128)(2,1)}, /*index=5*/bf16[256,256]{1,0:T(8,128)(2,1)}) custom-call(s32[2]{0:T(128)} %pad_add_fusion.me_ref, bf16[256,2048]{1,0:T(8,128)(2,1)} %bitcast.129, f32[1,2048]{1,0:T(1,128)} %bitcast.159, ...), custom_call_target="tpu_custom_call" | custom-call | flops 134217728 | bytes 984192 | tf_op jit(solution)/shard_map/pallas_call | solution.py:27
  65.2 4.6 %collective-permute-done.15.refs_7_ = bf16[2,256,256]{2,1,0:T(8,128)(2,1)} collective-permute-done((bf16[2,256,256]{2,1,0:T(8,128)(2,1)S(1)}, bf16[2,256,256]{2,1,0:T(8,128)(2,1)}, u32[]{:S(2)}, u32[]{:S(2)}) %collective-permute-start.15) | collective-permute-done | bytes 262176 | tf_op jit(solution)/shard_map/ppermute | solution.py:57
  73.2 4.8 %all-to-all-start.1 = ((bf16[4,64,2048]{2,1,0:T(8,128)(2,1)}), bf16[4,64,2048]{2,1,0:T(8,128)(2,1)S(1)}, u32[]{:S(2)}, u32[]{:S(2)}) async-start(bf16[4,64,2048]{2,1,0:T(8,128)(2,1)} %broadcast_in_dim.59), calls=%async_computation.1 | async-start | bytes 2097152 | tf_op jit(solution)/shard_map/all_to_all | solution.py:109
  83.3 8.0 %shard_map.255 = (f32[256,512]{1,0:T(8,128)}, f32[256,512]{1,0:T(8,128)}, bf16[256,512]{1,0:T(8,128)(2,1)}, bf16[4,64,2048]{2,1,0:T(8,128)(2,1)}) custom-call(bf16[256,512]{1,0:T(8,128)(2,1)} %get-tuple-element.113.q, bf16[256,2048]{1,0:T(8,128)(2,1)} %get-tuple-element.157.normed_ref, s32[256,1]{1,0:T(8,128)} %copy.55.qpos, s32[1,1024]{1,0:T(1,128)} %bitcast.161, ...), custom_call_target="tpu_custom_call" | custom-call | flops 201326592 | bytes 1245824 | tf_op jit(solution)/shard_map/pallas_call | solution.py:27
  91.3 13.1 %all-to-all-done.1 = bf16[4,64,2048]{2,1,0:T(8,128)(2,1)S(1)} async-done(((bf16[4,64,2048]{2,1,0:T(8,128)(2,1)}), bf16[4,64,2048]{2,1,0:T(8,128)(2,1)S(1)}, u32[]{:S(2)}, u32[]{:S(2)}) %all-to-all-start.1) | async-done | bytes 1048608 | tf_op jit(solution)/shard_map/all_to_all | solution.py:109
  104.4 4.3 all-to-all-start.2
  117.3 16.9 %all-to-all-done.2.got_ref = bf16[4,64,2048]{2,1,0:T(8,128)(2,1)} async-done(((bf16[4,64,2048]{2,1,0:T(8,128)(2,1)}), bf16[4,64,2048]{2,1,0:T(8,128)(2,1)}, u32[]{:S(2)}, u32[]{:S(2)}) %all-to-all-start.2) | async-done | bytes 1048608 | tf_op jit(solution)/shard_map/all_to_all | solution.py:109
  137.1 14.5 %all-to-all-start.3 = ((bf16[4,64,2048]{2,1,0:T(8,128)(2,1)}), bf16[4,64,2048]{2,1,0:T(8,128)(2,1)S(1)}, u32[]{:S(2)}, u32[]{:S(2)}) async-start(bf16[4,64,2048]{2,1,0:T(8,128)(2,1)} %get-tuple-element.121), calls=%async_computation.3 | async-start | bytes 2097152 | tf_op jit(solution)/shard_map/all_to_all | solution.py:109
  152.2 12.2 %collective-permute-done.30.r_6_.r_10_ = bf16[2,3,96,2048]{3,2,1,0:T(8,128)(2,1)} collective-permute-done((bf16[2,3,96,2048]{3,2,1,0:T(8,128)(2,1)}, bf16[2,3,96,2048]{3,2,1,0:T(8,128)(2,1)}, u32[]{:S(2)}, u32[]{:S(2)}) %collective-permute-start.30) | collective-permute-done | bytes 2359328 | tf_op jit(solution)/shard_map/ppermute | solution.py:57
  164.4 12.2 %all-to-all-done.3 = bf16[4,64,2048]{2,1,0:T(8,128)(2,1)S(1)} async-done(((bf16[4,64,2048]{2,1,0:T(8,128)(2,1)}), bf16[4,64,2048]{2,1,0:T(8,128)(2,1)S(1)}, u32[]{:S(2)}, u32[]{:S(2)}) %all-to-all-start.3) | async-done | bytes 1048608 | tf_op jit(solution)/shard_map/all_to_all | solution.py:109
  177.6 8.2 %shard_map.257 = (f32[768,256]{1,0:T(8,128)}, f32[768,256]{1,0:T(8,128)}, bf16[768,256]{1,0:T(8,128)(2,1)}, f32[256,2048]{1,0:T(8,128)}) custom-call(bf16[256,2048]{1,0:T(8,128)(2,1)} %bitcast.107, bf16[1,3,96,2048]{3,2,1,0:T(8,128)(2,1)} %copy-done.2, bf16[1,3,96,2048]{3,2,1,0:T(8,128)(2,1)} %collective-permute-done.24.r_2_.r_6_, ...), custom_call_target="tpu_custom_call" | custom-call | flops 301989888 | bytes 1441792 | tf_op jit(solution)/shard_map/pallas_call | solution.py:452
  187.2 8.5 %shard_map.258 = (f32[768,256]{1,0:T(8,128)}, f32[768,256]{1,0:T(8,128)}, bf16[768,256]{1,0:T(8,128)(2,1)}, bf16[256,2048]{1,0:T(8,128)(2,1)}) custom-call(bf16[256,2048]{1,0:T(8,128)(2,1)} %bitcast.108, bf16[2,3,96,2048]{3,2,1,0:T(8,128)(2,1)} %collective-permute-done.25.r_1_.r_5_, bf16[2,3,96,2048]{3,2,1,0:T(8,128)(2,1)} %collective-permute-done.27.r_2_.r_6_, ...), custom_call_target="tpu_custom_call" | custom-call | flops 301989888 | bytes 1441792 | tf_op jit(solution)/shard_map/pallas_call | solution.py:452
  195.7 3.5 all-to-all-start.4
  199.2 12.0 %shard_map.259 = (bf16[384,2048]{1,0:T(8,128)(2,1)}, bf16[384,2048]{1,0:T(8,128)(2,1)}, bf16[384,2048]{1,0:T(8,128)(2,1)}, bf16[384,2048]{1,0:T(8,128)(2,1)}, bf...) custom-call(bf16[256,2048]{1,0:T(8,128)(2,1)} %bitcast.109, bf16[256,2048]{1,0:T(8,128)(2,1)} %bitcast.113, ...), custom_call_target="tpu_custom_call" | custom-call | flops 603979776 | bytes 2883584 | tf_op jit(solution)/shard_map/pallas_call | solution.py:526
  212.4 12.3 %shard_map.260 = (bf16[384,2048]{1,0:T(8,128)(2,1)}, bf16[384,2048]{1,0:T(8,128)(2,1)}, bf16[384,2048]{1,0:T(8,128)(2,1)}, bf16[384,2048]{1,0:T(8,128)(2,1)}, bf...) custom-call(bf16[256,2048]{1,0:T(8,128)(2,1)} %bitcast.110, ...), custom_call_target="tpu_custom_call" | custom-call | flops 603979776 | bytes 2883584 | tf_op jit(solution)/shard_map/pallas_call | solution.py:526
  225.0 5.2 %all-to-all-start.5 = ((bf16[4,64,2048]{2,1,0:T(8,128)(2,1)}), bf16[4,64,2048]{2,1,0:T(8,128)(2,1)S(1)}, u32[]{:S(2)}, u32[]{:S(2)}) async-start(bf16[4,64,2048]{2,1,0:T(8,128)(2,1)} %bitcast.150), calls=%async_computation.5 | async-start | bytes 2097152 | tf_op jit(solution)/shard_map/all_to_all | solution.py:109
  236.3 3.3 add_convert_fusion.6
  244.4 3.2 add_convert_fusion.2
  262.9 5.0 %all-to-all-start.6 = ((bf16[4,64,2048]{2,1,0:T(8,128)(2,1)}), bf16[4,64,2048]{2,1,0:T(8,128)(2,1)S(1)}, u32[]{:S(2)}, u32[]{:S(2)}) async-start(bf16[4,64,2048]{2,1,0:T(8,128)(2,1)} %get-tuple-element.142), calls=%async_computation.6 | async-start | bytes 2097152 | tf_op jit(solution)/shard_map/all_to_all | solution.py:109
  268.7 12.0 %collective-permute-done.36 = bf16[96,2048]{1,0:T(8,128)(2,1)} collective-permute-done((bf16[96,2048]{1,0:T(8,128)(2,1)}, bf16[96,2048]{1,0:T(8,128)(2,1)}, u32[]{:S(2)}, u32[]{:S(2)}) %collective-permute-start.36) | collective-permute-done | bytes 393248 | tf_op jit(solution)/shard_map/ppermute | solution.py:57
  293.1 9.4 %shard_map.262 = (bf16[1024,256]{1,0:T(8,128)(2,1)}, bf16[1024,256]{1,0:T(8,128)(2,1)}, bf16[1024,256]{1,0:T(8,128)(2,1)}, bf16[1024,256]{1,0:T(8,128)(2,1)}, bf...) custom-call(bf16[256,512]{1,0:T(8,128)(2,1)} %get-tuple-element.113.q, ...), custom_call_target="tpu_custom_call" | custom-call | flops 234881024 | bytes 1377024 | tf_op jit(solution)/shard_map/pallas_call | solution.py:27
  306.0 4.5 %all-to-all-start.7 = ((bf16[4,192,512]{2,1,0:T(8,128)(2,1)}), bf16[4,192,512]{2,1,0:T(8,128)(2,1)}, u32[]{:S(2)}, u32[]{:S(2)}) async-start(bf16[4,192,512]{2,1,0:T(8,128)(2,1)} %maximum_bitcast_fusion.1), calls=%async_computation.7 | async-start | bytes 1572864 | tf_op jit(solution)/shard_map/all_to_all | solution.py:109
  326.3 4.0 collective-permute-done.69
  331.2 3.8 all-to-all-start.8
  337.7 7.3 %shard_map.263 = (bf16[1024,512]{1,0:T(8,128)(2,1)}, bf16[1024,512]{1,0:T(8,128)(2,1)}, bf16[1024,512]{1,0:T(8,128)(2,1)}, bf16[1024,512]{1,0:T(8,128)(2,1)}, bf...) custom-call(bf16[256,2048]{1,0:T(8,128)(2,1)} %get-tuple-element.157.normed_ref, ...), custom_call_target="tpu_custom_call" | custom-call | flops 335544320 | bytes 1933312 | tf_op jit(solution)/shard_map/pallas_call | solution.py:27
  349.1 5.9 %shard_map.264 = (bf16[1024,512]{1,0:T(8,128)(2,1)}, bf16[1024,512]{1,0:T(8,128)(2,1)}, f32[1,128]{1,0:T(1,128)}, bf16[4,64,2048]{2,1,0:T(8,128)(2,1)}) custom-call(f32[256,256]{1,0:T(8,128)} %convert_add_fusion.4.dk, f32[256,256]{1,0:T(8,128)} %convert_add_fusion.3.dv, f32[256,256]{1,0:T(8,128)} %get-tuple-element.156.kpre, ...), custom_call_target="tpu_custom_call" | custom-call | flops 134217728 | bytes 1179776 | tf_op jit(solution)/shard_map/pallas_call | solution.py:27
  358.8 5.1 %all-to-all-start.9 = ((bf16[4,64,2048]{2,1,0:T(8,128)(2,1)}), bf16[4,64,2048]{2,1,0:T(8,128)(2,1)S(1)}, u32[]{:S(2)}, u32[]{:S(2)}) async-start(bf16[4,64,2048]{2,1,0:T(8,128)(2,1)} %get-tuple-element.173), calls=%async_computation.9 | async-start | bytes 2097152 | tf_op jit(solution)/shard_map/all_to_all | solution.py:109
  378.6 7.1 %collective-permute-done.62 = bf16[512,512]{1,0:T(8,128)(2,1)S(1)} collective-permute-done((bf16[512,512]{1,0:T(8,128)(2,1)S(1)}, bf16[512,512]{1,0:T(8,128)(2,1)S(1)}, u32[]{:S(2)}, u32[]{:S(2)}) %collective-permute-start.62) | collective-permute-done | bytes 524320 | tf_op jit(solution)/shard_map/ppermute | solution.py:57
  401.6 4.9 %all-to-all-start.10 = ((bf16[4,192,512]{2,1,0:T(8,128)(2,1)}), bf16[4,192,512]{2,1,0:T(8,128)(2,1)S(1)}, u32[]{:S(2)}, u32[]{:S(2)}) async-start(bf16[4,192,512]{2,1,0:T(8,128)(2,1)} %maximum_bitcast_fusion.3), calls=%async_computation.10 | async-start | bytes 1572864 | tf_op jit(solution)/shard_map/all_to_all | solution.py:109
  411.9 5.4 %collective-permute-done.53 = f32[34,128]{1,0:T(8,128)S(1)} collective-permute-done((f32[34,128]{1,0:T(8,128)S(1)}, f32[34,128]{1,0:T(8,128)S(1)}, u32[]{:S(2)}, u32[]{:S(2)}) %collective-permute-start.53) | collective-permute-done | bytes 17440 | tf_op jit(solution)/shard_map/ppermute | solution.py:57
  (372 shorter events, 183.7 us)
Async XLA Ops:
  14.3 57.8 %all-to-all-start = ((bf16[4,3,192,512]{3,2,1,0:T(8,128)(2,1)}), bf16[4,3,192,512]{3,2,1,0:T(8,128)(2,1)S(1)}, u32[]{:S(2)}, u32[]{:S(2)}) async-start(bf16[4,3,192,512]{3,2,1,0:T(8,128)(2,1)} %copy.54), calls=%async_computation | async-start | bytes 4718592 | tf_op jit(solution)/shard_map/all_to_all | solution.py:109
  73.2 31.2 %all-to-all-start.1 = ((bf16[4,64,2048]{2,1,0:T(8,128)(2,1)}), bf16[4,64,2048]{2,1,0:T(8,128)(2,1)S(1)}, u32[]{:S(2)}, u32[]{:S(2)}) async-start(bf16[4,64,2048]{2,1,0:T(8,128)(2,1)} %broadcast_in_dim.59), calls=%async_computation.1 | async-start | bytes 2097152 | tf_op jit(solution)/shard_map/all_to_all | solution.py:109
  78.6 30.1 %collective-permute-start.28 = (bf16[1,3,96,2048]{3,2,1,0:T(8,128)(2,1)S(1)}, bf16[1,3,96,2048]{3,2,1,0:T(8,128)(2,1)}, u32[]{:S(2)}, u32[]{:S(2)}) collective-permute-start(bf16[1,3,96,2048]{3,2,1,0:T(8,128)(2,1)S(1)} %get-tuple-element.264.r_4_.r_8_), channel_id=1, source_target_pairs={{0,16},{4,20},{8,24},{12,28},{16,0},{20,4},{24,8},{28,12},{1,17},{... | collective-permute-start | bytes 3538952 | tf_op jit(solution)/shard_map/ppermute | solution.py:57
  79.2 32.9 %collective-permute-start.24 = (bf16[1,3,96,2048]{3,2,1,0:T(8,128)(2,1)S(1)}, bf16[1,3,96,2048]{3,2,1,0:T(8,128)(2,1)}, u32[]{:S(2)}, u32[]{:S(2)}) collective-permute-start(bf16[1,3,96,2048]{3,2,1,0:T(8,128)(2,1)S(1)} %get-tuple-element.265.r_1_.r_5_), channel_id=1, source_target_pairs={{0,8},{4,12},{8,0},{12,4},{16,24},{20,28},{24,16},{28,20},{1,9},{5... | collective-permute-start | bytes 3538952 | tf_op jit(solution)/shard_map/ppermute | solution.py:57
  104.4 29.9 %all-to-all-start.2 = ((bf16[4,64,2048]{2,1,0:T(8,128)(2,1)}), bf16[4,64,2048]{2,1,0:T(8,128)(2,1)}, u32[]{:S(2)}, u32[]{:S(2)}) async-start(bf16[4,64,2048]{2,1,0:T(8,128)(2,1)} %get-tuple-element.119), calls=%async_computation.2 | async-start | bytes 2097152 | tf_op jit(solution)/shard_map/all_to_all | solution.py:109
  111.5 52.8 %collective-permute-start.30 = (bf16[2,3,96,2048]{3,2,1,0:T(8,128)(2,1)}, bf16[2,3,96,2048]{3,2,1,0:T(8,128)(2,1)}, u32[]{:S(2)}, u32[]{:S(2)}) collective-permute-start(bf16[2,3,96,2048]{3,2,1,0:T(8,128)(2,1)} %pad_maximum_fusion.1), channel_id=1, source_target_pairs={{0,8},{4,12},{8,0},{12,4},{16,24},{20,28},{24,16},{28,20},{1,9},{5... | collective-permute-start | bytes 7077896 | tf_op jit(solution)/shard_map/ppermute | solution.py:57
  115.0 61.6 %collective-permute-start.26 = (bf16[2,3,96,2048]{3,2,1,0:T(8,128)(2,1)}, bf16[2,3,96,2048]{3,2,1,0:T(8,128)(2,1)}, u32[]{:S(2)}, u32[]{:S(2)}) collective-permute-start(bf16[2,3,96,2048]{3,2,1,0:T(8,128)(2,1)} %pad_maximum_fusion), channel_id=1, source_target_pairs={{0,16},{4,20},{8,24},{12,28},{16,0},{20,4},{24,8},{28,12},{1,17},{... | collective-permute-start | bytes 7077896 | tf_op jit(solution)/shard_map/ppermute | solution.py:57
  137.1 39.5 %all-to-all-start.3 = ((bf16[4,64,2048]{2,1,0:T(8,128)(2,1)}), bf16[4,64,2048]{2,1,0:T(8,128)(2,1)S(1)}, u32[]{:S(2)}, u32[]{:S(2)}) async-start(bf16[4,64,2048]{2,1,0:T(8,128)(2,1)} %get-tuple-element.121), calls=%async_computation.3 | async-start | bytes 2097152 | tf_op jit(solution)/shard_map/all_to_all | solution.py:109
  151.7 34.1 %collective-permute-start.29 = (bf16[2,3,96,2048]{3,2,1,0:T(8,128)(2,1)}, bf16[2,3,96,2048]{3,2,1,0:T(8,128)(2,1)S(1)}, u32[]{:S(2)}, u32[]{:S(2)}) collective-permute-start(bf16[2,3,96,2048]{3,2,1,0:T(8,128)(2,1)} %pad_maximum_fusion.1), channel_id=1, source_target_pairs={{0,4},{4,0},{8,12},{12,8},{16,20},{20,16},{24,28},{28,24},{1,5},{5... | collective-permute-start | bytes 7077896 | tf_op jit(solution)/shard_map/ppermute | solution.py:57
  151.7 34.1 %collective-permute-start.25 = (bf16[2,3,96,2048]{3,2,1,0:T(8,128)(2,1)}, bf16[2,3,96,2048]{3,2,1,0:T(8,128)(2,1)}, u32[]{:S(2)}, u32[]{:S(2)}) collective-permute-start(bf16[2,3,96,2048]{3,2,1,0:T(8,128)(2,1)} %pad_maximum_fusion), channel_id=1, source_target_pairs={{0,4},{4,0},{8,12},{12,8},{16,20},{20,16},{24,28},{28,24},{1,5},{5... | collective-permute-start | bytes 7077896 | tf_op jit(solution)/shard_map/ppermute | solution.py:57
  195.7 29.3 %all-to-all-start.4 = ((bf16[4,64,2048]{2,1,0:T(8,128)(2,1)}), bf16[4,64,2048]{2,1,0:T(8,128)(2,1)S(1)}, u32[]{:S(2)}, u32[]{:S(2)}) async-start(bf16[4,64,2048]{2,1,0:T(8,128)(2,1)} %bitcast.151), calls=%async_computation.4 | async-start | bytes 2097152 | tf_op jit(solution)/shard_map/all_to_all | solution.py:109
  211.8 23.9 %collective-permute-start.44 = (bf16[384,2048]{1,0:T(8,128)(2,1)}, bf16[384,2048]{1,0:T(8,128)(2,1)}, u32[]{:S(2)}, u32[]{:S(2)}) collective-permute-start(bf16[384,2048]{1,0:T(8,128)(2,1)} %get-tuple-element.165), channel_id=1, source_target_pairs={{0,4},{4,0},{8,12},{12,8},{16,20},{20,16},{24,28},{28,24},{1,5},{5... | collective-permute-start | bytes 4718600 | tf_op jit(solution)/shard_map/ppermute | solution.py:57
  211.9 31.0 %collective-permute-start.67 = (bf16[384,2048]{1,0:T(8,128)(2,1)}, bf16[384,2048]{1,0:T(8,128)(2,1)}, u32[]{:S(2)}, u32[]{:S(2)}) collective-permute-start(bf16[384,2048]{1,0:T(8,128)(2,1)} %get-tuple-element.194), channel_id=1, source_target_pairs={{0,4},{4,0},{8,12},{12,8},{16,20},{20,16},{24,28},{28,24},{1,5},{5... | collective-permute-start | bytes 4718600 | tf_op jit(solution)/shard_map/ppermute | solution.py:57
  212.3 35.3 %collective-permute-start.70 = (bf16[384,2048]{1,0:T(8,128)(2,1)}, bf16[384,2048]{1,0:T(8,128)(2,1)}, u32[]{:S(2)}, u32[]{:S(2)}) collective-permute-start(bf16[384,2048]{1,0:T(8,128)(2,1)} %get-tuple-element.200), channel_id=1, source_target_pairs={{0,4},{4,0},{8,12},{12,8},{16,20},{20,16},{24,28},{28,24},{1,5},{5... | collective-permute-start | bytes 4718600 | tf_op jit(solution)/shard_map/ppermute | solution.py:57
  225.0 33.7 %all-to-all-start.5 = ((bf16[4,64,2048]{2,1,0:T(8,128)(2,1)}), bf16[4,64,2048]{2,1,0:T(8,128)(2,1)S(1)}, u32[]{:S(2)}, u32[]{:S(2)}) async-start(bf16[4,64,2048]{2,1,0:T(8,128)(2,1)} %bitcast.150), calls=%async_computation.5 | async-start | bytes 2097152 | tf_op jit(solution)/shard_map/all_to_all | solution.py:109
  239.6 46.3 %collective-permute-start.45 = (bf16[192,2048]{1,0:T(8,128)(2,1)}, bf16[192,2048]{1,0:T(8,128)(2,1)}, u32[]{:S(2)}, u32[]{:S(2)}) collective-permute-start(bf16[192,2048]{1,0:T(8,128)(2,1)} %get-tuple-element.256), channel_id=1, source_target_pairs={{0,8},{4,12},{8,0},{12,4},{16,24},{20,28},{24,16},{28,20},{1,9},{5... | collective-permute-start | bytes 2359304 | tf_op jit(solution)/shard_map/ppermute | solution.py:57
  242.9 46.4 %collective-permute-start.48 = (bf16[192,2048]{1,0:T(8,128)(2,1)}, bf16[192,2048]{1,0:T(8,128)(2,1)}, u32[]{:S(2)}, u32[]{:S(2)}) collective-permute-start(bf16[192,2048]{1,0:T(8,128)(2,1)} %get-tuple-element.258), channel_id=1, source_target_pairs={{0,16},{4,20},{8,24},{12,28},{16,0},{20,4},{24,8},{28,12},{1,17},{... | collective-permute-start | bytes 2359304 | tf_op jit(solution)/shard_map/ppermute | solution.py:57
  254.5 26.2 %collective-permute-start.36 = (bf16[96,2048]{1,0:T(8,128)(2,1)}, bf16[96,2048]{1,0:T(8,128)(2,1)}, u32[]{:S(2)}, u32[]{:S(2)}) collective-permute-start(bf16[96,2048]{1,0:T(8,128)(2,1)} %add_convert_fusion.36), channel_id=1, source_target_pairs={{0,16},{4,20},{8,24},{12,28},{16,0},{20,4},{24,8},{28,12},{1,17},{... | collective-permute-start | bytes 1179656 | tf_op jit(solution)/shard_map/ppermute | solution.py:57
  257.2 23.5 %collective-permute-start.39 = (bf16[96,2048]{1,0:T(8,128)(2,1)}, bf16[96,2048]{1,0:T(8,128)(2,1)}, u32[]{:S(2)}, u32[]{:S(2)}) collective-permute-start(bf16[96,2048]{1,0:T(8,128)(2,1)} %add_convert_fusion.33), channel_id=1, source_target_pairs={{0,8},{4,12},{8,0},{12,4},{16,24},{20,28},{24,16},{28,20},{1,9},{5... | collective-permute-start | bytes 1179656 | tf_op jit(solution)/shard_map/ppermute | solution.py:57
  262.9 29.3 %all-to-all-start.6 = ((bf16[4,64,2048]{2,1,0:T(8,128)(2,1)}), bf16[4,64,2048]{2,1,0:T(8,128)(2,1)S(1)}, u32[]{:S(2)}, u32[]{:S(2)}) async-start(bf16[4,64,2048]{2,1,0:T(8,128)(2,1)} %get-tuple-element.142), calls=%async_computation.6 | async-start | bytes 2097152 | tf_op jit(solution)/shard_map/all_to_all | solution.py:109
  283.9 31.8 %collective-permute-start.68 = (bf16[192,2048]{1,0:T(8,128)(2,1)}, bf16[192,2048]{1,0:T(8,128)(2,1)}, u32[]{:S(2)}, u32[]{:S(2)}) collective-permute-start(bf16[192,2048]{1,0:T(8,128)(2,1)} %get-tuple-element.196), channel_id=1, source_target_pairs={{0,8},{4,12},{8,0},{12,4},{16,24},{20,28},{24,16},{28,20},{1,9},{5... | collective-permute-start | bytes 2359304 | tf_op jit(solution)/shard_map/ppermute | solution.py:57
  285.4 32.7 %collective-permute-start.71 = (bf16[192,2048]{1,0:T(8,128)(2,1)}, bf16[192,2048]{1,0:T(8,128)(2,1)}, u32[]{:S(2)}, u32[]{:S(2)}) collective-permute-start(bf16[192,2048]{1,0:T(8,128)(2,1)} %get-tuple-element.202), channel_id=1, source_target_pairs={{0,16},{4,20},{8,24},{12,28},{16,0},{20,4},{24,8},{28,12},{1,17},{... | collective-permute-start | bytes 2359304 | tf_op jit(solution)/shard_map/ppermute | solution.py:57
  287.8 33.8 %collective-permute-start.46 = (bf16[96,2048]{1,0:T(8,128)(2,1)}, bf16[96,2048]{1,0:T(8,128)(2,1)}, u32[]{:S(2)}, u32[]{:S(2)}) collective-permute-start(bf16[96,2048]{1,0:T(8,128)(2,1)} %add_convert_fusion.30), channel_id=1, source_target_pairs={{0,16},{4,20},{8,24},{12,28},{16,0},{20,4},{24,8},{28,12},{1,17},{... | collective-permute-start | bytes 1179656 | tf_op jit(solution)/shard_map/ppermute | solution.py:57
  306.0 25.2 %all-to-all-start.7 = ((bf16[4,192,512]{2,1,0:T(8,128)(2,1)}), bf16[4,192,512]{2,1,0:T(8,128)(2,1)}, u32[]{:S(2)}, u32[]{:S(2)}) async-start(bf16[4,192,512]{2,1,0:T(8,128)(2,1)} %maximum_bitcast_fusion.1), calls=%async_computation.7 | async-start | bytes 1572864 | tf_op jit(solution)/shard_map/all_to_all | solution.py:109
  321.5 27.0 %collective-permute-start.72 = (bf16[96,2048]{1,0:T(8,128)(2,1)}, bf16[96,2048]{1,0:T(8,128)(2,1)}, u32[]{:S(2)}, u32[]{:S(2)}) collective-permute-start(bf16[96,2048]{1,0:T(8,128)(2,1)} %add_convert_fusion.21), channel_id=1, source_target_pairs={{0,8},{4,12},{8,0},{12,4},{16,24},{20,28},{24,16},{28,20},{1,9},{5... | collective-permute-start | bytes 1179656 | tf_op jit(solution)/shard_map/ppermute | solution.py:57
  331.2 26.6 %all-to-all-start.8 = ((bf16[4,192,512]{2,1,0:T(8,128)(2,1)}), bf16[4,192,512]{2,1,0:T(8,128)(2,1)S(1)}, u32[]{:S(2)}, u32[]{:S(2)}) async-start(bf16[4,192,512]{2,1,0:T(8,128)(2,1)} %maximum_bitcast_fusion.2), calls=%async_computation.8 | async-start | bytes 1572864 | tf_op jit(solution)/shard_map/all_to_all | solution.py:109
  348.6 22.0 %collective-permute-start.61 = (bf16[1024,512]{1,0:T(8,128)(2,1)}, bf16[1024,512]{1,0:T(8,128)(2,1)S(1)}, u32[]{:S(2)}, u32[]{:S(2)}) collective-permute-start(bf16[1024,512]{1,0:T(8,128)(2,1)} %get-tuple-element.189), channel_id=1, source_target_pairs={{0,4},{4,0},{8,12},{12,8},{16,20},{20,16},{24,28},{28,24},{1,5},{5... | collective-permute-start | bytes 3145736 | tf_op jit(solution)/shard_map/ppermute | solution.py:57
  358.8 31.0 %all-to-all-start.9 = ((bf16[4,64,2048]{2,1,0:T(8,128)(2,1)}), bf16[4,64,2048]{2,1,0:T(8,128)(2,1)S(1)}, u32[]{:S(2)}, u32[]{:S(2)}) async-start(bf16[4,64,2048]{2,1,0:T(8,128)(2,1)} %get-tuple-element.173), calls=%async_computation.9 | async-start | bytes 2097152 | tf_op jit(solution)/shard_map/all_to_all | solution.py:109
  369.0 37.5 %collective-permute-start.65 = (bf16[512,512]{1,0:T(8,128)(2,1)}, bf16[512,512]{1,0:T(8,128)(2,1)}, u32[]{:S(2)}, u32[]{:S(2)}) collective-permute-start(bf16[512,512]{1,0:T(8,128)(2,1)} %get-tuple-element.266), channel_id=1, source_target_pairs={{0,16},{4,20},{8,24},{12,28},{16,0},{20,4},{24,8},{28,12},{1,17},{... | collective-permute-start | bytes 1572872 | tf_op jit(solution)/shard_map/ppermute | solution.py:57
  374.5 34.3 %collective-permute-start.59 = (bf16[512,512]{1,0:T(8,128)(2,1)}, bf16[512,512]{1,0:T(8,128)(2,1)}, u32[]{:S(2)}, u32[]{:S(2)}) collective-permute-start(bf16[512,512]{1,0:T(8,128)(2,1)} %get-tuple-element.270), channel_id=1, source_target_pairs={{0,16},{4,20},{8,24},{12,28},{16,0},{20,4},{24,8},{28,12},{1,17},{... | collective-permute-start | bytes 1572872 | tf_op jit(solution)/shard_map/ppermute | solution.py:57
  377.5 34.4 %collective-permute-start.56 = (bf16[512,512]{1,0:T(8,128)(2,1)}, bf16[512,512]{1,0:T(8,128)(2,1)}, u32[]{:S(2)}, u32[]{:S(2)}) collective-permute-start(bf16[512,512]{1,0:T(8,128)(2,1)} %get-tuple-element.272), channel_id=1, source_target_pairs={{0,8},{4,12},{8,0},{12,4},{16,24},{20,28},{24,16},{28,20},{1,9},{5... | collective-permute-start | bytes 1572872 | tf_op jit(solution)/shard_map/ppermute | solution.py:57
  401.6 27.3 %all-to-all-start.10 = ((bf16[4,192,512]{2,1,0:T(8,128)(2,1)}), bf16[4,192,512]{2,1,0:T(8,128)(2,1)S(1)}, u32[]{:S(2)}, u32[]{:S(2)}) async-start(bf16[4,192,512]{2,1,0:T(8,128)(2,1)} %maximum_bitcast_fusion.3), calls=%async_computation.10 | async-start | bytes 1572864 | tf_op jit(solution)/shard_map/all_to_all | solution.py:109
  (116 other events, 1153.6 us)
